TPU v7x, 512 devices: a whole 4x8x8 slice. The times are simulated.
512 devices in a mesh: blk: 64 (over y_lo, z, x), row: 8 (over y_hi, core).
Axes of the slice: x: 4, y: 8 (y_hi: 4, y_lo: 2; y = y_hi * 2 + y_lo), z: 8, core: 2. Of those that a mesh axis runs over, the one named last changes fastest.
Arguments:
- points: bfloat16 [65536, 128], P(('blk', 'row')), may hold values from -6 to 6
- w_in: bfloat16 [128, 1024], replicated, may hold values from -0.5 to 0.5
- b_in: float32 [1024], replicated, may hold values from -4 to 4
- w_out: bfloat16 [1024, 128], replicated, may hold values from -0.1875 to 0.1875
- scales: float32 [128], replicated, may hold values from 0.04 to 0.16
- left: bfloat16 [65536, 64], P(('blk', 'row')), may hold values from -2 to 2
- right: bfloat16 [65536, 64], P(('blk', 'row')), may hold values from -2 to 2
Outputs:
- feat_grad: float32 [65536, 128], P(('blk', 'row'))
- grad_w_in: float32 [128, 1024], replicated
- grad_b_in: float32 [1024], replicated
- grad_w_out: float32 [1024, 128], replicated
All inputs are finite; a program needn't handle non-finite values.
Results may differ from a plain program's by a relative error of at most 0.012.
The roundings to bfloat16 on the way count: a program that leaves them out, or rounds other values in their place, can miss the bound.
Values may be sent and summed in bfloat16 or wider, within the bound.
A program may use at most 64 MiB of HBM per device.

v0:
```python
import jax
import jax.numpy as jnp
from jax import lax
from jax.sharding import PartitionSpec as P


def sent_together(arrays, axis, dim, along):
    widths = [a.shape[along] for a in arrays]
    both = jnp.concatenate(arrays, axis=along)
    result = lax.all_gather(both, axis, axis=dim, tiled=True)
    return tuple(jnp.split(result, [sum(widths[:k]) for k in range(1, len(widths))], axis=along))


def from_behind(value, axis, steps):
    count = lax.axis_size(axis)
    pairs = [(source, (source + steps) % count) for source in range(count)]
    return lax.ppermute(value, axis, pairs)


def cut_along(array, dim, devices):
    lengths = array.shape
    blocks = array.reshape(*lengths[:dim], devices, lengths[dim] // devices, *lengths[dim + 1 :])
    return jnp.moveaxis(blocks, dim, 0)


def sum_at_owner(array, axis, dim):
    blocks = cut_along(array, dim, lax.axis_size(axis))
    arrived = lax.all_to_all(blocks, axis, split_axis=0, concat_axis=0, tiled=True)
    return arrived.sum(axis=0)


def silu_slope(pre):
    sig = jax.nn.sigmoid(pre)
    return sig * (1.0 + pre * (1.0 - sig))


def local(points, w_in, b_in, w_out, scales, left, right):
    pre = jnp.dot(points, w_in, preferred_element_type=jnp.float32) + b_in
    hidden = jax.nn.silu(pre).astype(jnp.bfloat16)
    feats = jnp.dot(hidden, w_out, preferred_element_type=jnp.float32)
    scaled = (feats * scales).astype(jnp.bfloat16)
    pairs_ab = jnp.concatenate([left, right], axis=1)
    pairs_ba = jnp.concatenate([right, left], axis=1)
    home_g, home_ab = sent_together((scaled, pairs_ab), "row", 0, 1)
    home_f = home_g.astype(jnp.float32)
    home_n = jnp.sum(home_f * home_f, axis=1)
    contract = (((1,), (1,)), ((), ()))
    down = (((0,), (0,)), ((), ()))

    def tile(visit_g, visit_ba):
        visit_f = visit_g.astype(jnp.float32)
        visit_n = jnp.sum(visit_f * visit_f, axis=1)
        cross = lax.dot_general(visit_g, home_g, contract, preferred_element_type=jnp.float32)
        kern = jnp.exp(-0.5 * (visit_n[:, None] + home_n[None, :] - 2.0 * cross))
        coup = lax.dot_general(visit_ba, home_ab, contract, preferred_element_type=jnp.float32)
        weight = coup * kern
        weight_b = weight.astype(jnp.bfloat16)
        home_term = -jnp.sum(weight, axis=0)[:, None] * home_f + lax.dot_general(
            weight_b, visit_g, down, preferred_element_type=jnp.float32
        )
        visit_term = -jnp.sum(weight, axis=1)[:, None] * visit_f + jnp.dot(
            weight_b, home_g, preferred_element_type=jnp.float32
        )
        return (home_term, visit_term)

    home_acc, unused = tile(scaled, pairs_ba)
    blocks = lax.axis_size("blk")
    half = blocks // 2

    def visit_step(step, carry):
        visit_g, visit_ba, visit_acc, total = carry
        visit_g, visit_ba, visit_acc = (
            from_behind(visit_g.astype(jnp.float32), "blk", 1).astype(visit_g.dtype),
            from_behind(visit_ba.astype(jnp.float32), "blk", 1).astype(visit_ba.dtype),
            from_behind(visit_acc, "blk", 1),
        )
        home_term, visit_term = tile(visit_g, visit_ba)
        keep = (step < half).astype(jnp.float32)
        return (visit_g, visit_ba, visit_acc + keep * visit_term, total + home_term)

    start = (scaled, pairs_ba, jnp.zeros(feats.shape, jnp.float32), home_acc)
    unused_g, unused_ba, visit_acc, home_acc = lax.fori_loop(1, half + 1, visit_step, start)
    carried = from_behind(visit_acc, "blk", -half)
    own_sum = sum_at_owner(home_acc, "row", 0)
    feat_grad = (own_sum + carried) * scales
    feat_grad_b = feat_grad.astype(jnp.bfloat16)
    part_w_out = jnp.dot(hidden.T, feat_grad_b, preferred_element_type=jnp.float32)
    pre_grad = jnp.dot(feat_grad_b, w_out.T, preferred_element_type=jnp.float32) * silu_slope(pre)
    pre_grad_b = pre_grad.astype(jnp.bfloat16)
    part_w_in = jnp.dot(points.T, pre_grad_b, preferred_element_type=jnp.float32)
    part_b_in = jnp.sum(pre_grad, axis=0)
    grad_w_in, grad_b_in, grad_w_out = lax.psum((part_w_in, part_b_in, part_w_out), ("blk", "row"))
    factor = (points.shape[0] * blocks * lax.axis_size("row")) ** (-0.5)
    return (feat_grad, factor * grad_w_in, factor * grad_b_in, factor * grad_w_out)


def solution(mesh):
    placed = (
        P(("blk", "row"), None),
        P(),
        P(),
        P(),
        P(),
        P(("blk", "row"), None),
        P(("blk", "row"), None),
    )
    return jax.shard_map(
        local,
        mesh=mesh,
        in_specs=placed,
        out_specs=(P(("blk", "row"), None), P(), P(), P()),
        check_vma=False,
    )
```

profile of v0, /device:TPU:1, one launch (start us, length us, event | category | flops | bytes accessed | tf_op | source)
XLA Modules:
  0.0 814.1 jit_solution(11493214395384115716)
XLA Ops:
  10.8 21.6 %all_gather.3 = bf16[1024,256]{0,1:T(8,128)(2,1)S(1)} all-gather(bf16[128,256]{0,1:T(8,128)(2,1)S(1)} %pad_maximum_fusion), channel_id=1, replica_groups=mesh['blk'=64,'row'=8] {'row'}, dimensions={0}, use_global_device_ids=true | all-gather | bytes 589824 | tf_op jit(solution)/shard_map/all_gather | solution.py:10
  35.1 441.6 %while.20 = (s32[]{:T(128)}, bf16[128,128]{1,0:T(8,128)(2,1)S(1)}, bf16[128,128]{1,0:T(8,128)(2,1)S(1)}, f32[128,128]{1,0:T(8,128)S(1)}, f32[1024,128]{1,0:T(8,1...) while((s32[]{:T(128)}, bf16[128,128]{1,0:T(8,128)(2,1)S(1)}, ...), condition=%wide.region_7.8_spmd.clone, body=%wide.region_3.7_spmd.clone.sunk | while | flops 135806848 | bytes 5299465 | solution.py:82
  38.0 3.1 collective-permute-start.1
  44.0 5.3 collective-permute-done
  59.9 3.1 collective-permute-done
  73.5 3.1 collective-permute-done
  87.4 3.1 collective-permute-done
  101.0 3.1 collective-permute-done
  114.7 3.1 collective-permute-done
  168.8 3.1 collective-permute-done
  182.4 3.1 collective-permute-done
  195.9 3.1 collective-permute-done
  210.1 3.4 collective-permute-done
  237.3 3.1 collective-permute-done
  250.8 3.1 collective-permute-done
  332.8 3.1 collective-permute-done
  359.9 3.7 collective-permute-done
  387.0 3.4 collective-permute-done
  400.5 3.1 collective-permute-done
  441.7 3.1 collective-permute-done
  476.7 39.2 %all-to-all-start = ((f32[8,128,128]{2,1,0:T(8,128)}), f32[8,128,128]{2,1,0:T(8,128)S(1)}, u32[]{:S(2)}, u32[]{:S(2)}) async-start(f32[8,128,128]{2,1,0:T(8,128)} %bitcast), calls=%async_computation | async-start | bytes 1048576 | tf_op jit(solution)/shard_map/all_to_all | solution.py:28
  518.3 12.7 %all-to-all-done = f32[8,128,128]{2,1,0:T(8,128)S(1)} async-done(((f32[8,128,128]{2,1,0:T(8,128)}), f32[8,128,128]{2,1,0:T(8,128)S(1)}, u32[]{:S(2)}, u32[]{:S(2)}) %all-to-all-start) | async-done | bytes 524320 | tf_op jit(solution)/shard_map/all_to_all | solution.py:28
  534.6 97.2 %psum.22 = f32[1024]{0:T(1024)S(1)} all-reduce(f32[1024]{0:T(1024)S(1)} %get-tuple-element.247), channel_id=1, replica_groups=mesh['blk'=64,'row'=8] {'blk','row'}, use_global_device_ids=true, to_apply=%region_11.12 | all-reduce | flops 1024 | bytes 8192 | tf_op jit(solution)/shard_map/psum | solution.py:92
  632.4 171.9 %all-reduce.3.cloned.1.call-done = (f32[128,1024]{0,1:T(8,128)}, f32[1024,128]{1,0:T(8,128)}) async-done(((f32[128,1024]{0,1:T(8,128)}, f32[1024,128]{1,0:T(8,128)}), (f32[128,1024]{0,1:T(8,128)}, f32[1024,128]{1,0:T(8,128)})) %all-reduce.3.cloned.1.call-update) | async-done | bytes 1048592 | tf_op jit(solution)/shard_map/psum | solution.py:92
  (542 shorter events, 395.4 us)
Async XLA Ops:
  35.1 14.2 %collective-permute-start = (bf16[128,128]{1,0:T(8,128)(2,1)S(1)}, bf16[128,128]{1,0:T(8,128)(2,1)S(1)}, u32[]{:S(2)}, u32[]{:S(2)}) collective-permute-start(bf16[128,128]{1,0:T(8,128)(2,1)S(1)} %get-tuple-element.330), channel_id=1, source_target_pairs={{0,8},{8,16},{16,24},{24,32},{32,40},{40,48},{48,56},{56,64},{64,7... | collective-permute-start | bytes 98312 | tf_op jit(solution)/shard_map/while/body/eval_jaxpr/ppermute | solution.py:17
  38.0 13.2 %collective-permute-start.1 = (bf16[128,128]{1,0:T(8,128)(2,1)S(1)}, bf16[128,128]{1,0:T(8,128)(2,1)S(1)}, u32[]{:S(2)}, u32[]{:S(2)}) collective-permute-start(bf16[128,128]{1,0:T(8,128)(2,1)S(1)} %get-tuple-element.331), channel_id=1, source_target_pairs={{0,8},{8,16},{16,24},{24,32},{32,40},{40,48},{48,56},{56,64},{64,7... | collective-permute-start | bytes 98312 | tf_op jit(solution)/shard_map/while/body/eval_jaxpr/ppermute | solution.py:17
  41.2 12.7 %collective-permute-start.2 = (f32[128,128]{1,0:T(8,128)S(1)}, f32[128,128]{1,0:T(8,128)S(1)}, u32[]{:S(2)}, u32[]{:S(2)}) collective-permute-start(f32[128,128]{1,0:T(8,128)S(1)} %broadcast_select_fusion.2), channel_id=1, source_target_pairs={{0,8},{8,16},{16,24},{24,32},{32,40},{40,48},{48,56},{56,64},{64,7... | collective-permute-start | bytes 196616 | tf_op jit(solution)/shard_map/while/body/eval_jaxpr/ppermute | solution.py:17
  58.0 9.4 %collective-permute-start.2 = (f32[128,128]{1,0:T(8,128)S(1)}, f32[128,128]{1,0:T(8,128)S(1)}, u32[]{:S(2)}, u32[]{:S(2)}) collective-permute-start(f32[128,128]{1,0:T(8,128)S(1)} %broadcast_select_fusion.2), channel_id=1, source_target_pairs={{0,8},{8,16},{16,24},{24,32},{32,40},{40,48},{48,56},{56,64},{64,7... | collective-permute-start | bytes 196616 | tf_op jit(solution)/shard_map/while/body/eval_jaxpr/ppermute | solution.py:17
  71.5 9.8 %collective-permute-start.2 = (f32[128,128]{1,0:T(8,128)S(1)}, f32[128,128]{1,0:T(8,128)S(1)}, u32[]{:S(2)}, u32[]{:S(2)}) collective-permute-start(f32[128,128]{1,0:T(8,128)S(1)} %broadcast_select_fusion.2), channel_id=1, source_target_pairs={{0,8},{8,16},{16,24},{24,32},{32,40},{40,48},{48,56},{56,64},{64,7... | collective-permute-start | bytes 196616 | tf_op jit(solution)/shard_map/while/body/eval_jaxpr/ppermute | solution.py:17
  85.5 9.4 %collective-permute-start.2 = (f32[128,128]{1,0:T(8,128)S(1)}, f32[128,128]{1,0:T(8,128)S(1)}, u32[]{:S(2)}, u32[]{:S(2)}) collective-permute-start(f32[128,128]{1,0:T(8,128)S(1)} %broadcast_select_fusion.2), channel_id=1, source_target_pairs={{0,8},{8,16},{16,24},{24,32},{32,40},{40,48},{48,56},{56,64},{64,7... | collective-permute-start | bytes 196616 | tf_op jit(solution)/shard_map/while/body/eval_jaxpr/ppermute | solution.py:17
  99.0 9.6 %collective-permute-start.2 = (f32[128,128]{1,0:T(8,128)S(1)}, f32[128,128]{1,0:T(8,128)S(1)}, u32[]{:S(2)}, u32[]{:S(2)}) collective-permute-start(f32[128,128]{1,0:T(8,128)S(1)} %broadcast_select_fusion.2), channel_id=1, source_target_pairs={{0,8},{8,16},{16,24},{24,32},{32,40},{40,48},{48,56},{56,64},{64,7... | collective-permute-start | bytes 196616 | tf_op jit(solution)/shard_map/while/body/eval_jaxpr/ppermute | solution.py:17
  112.7 9.4 %collective-permute-start.2 = (f32[128,128]{1,0:T(8,128)S(1)}, f32[128,128]{1,0:T(8,128)S(1)}, u32[]{:S(2)}, u32[]{:S(2)}) collective-permute-start(f32[128,128]{1,0:T(8,128)S(1)} %broadcast_select_fusion.2), channel_id=1, source_target_pairs={{0,8},{8,16},{16,24},{24,32},{32,40},{40,48},{48,56},{56,64},{64,7... | collective-permute-start | bytes 196616 | tf_op jit(solution)/shard_map/while/body/eval_jaxpr/ppermute | solution.py:17
  192.0 9.5 %collective-permute-start.1 = (bf16[128,128]{1,0:T(8,128)(2,1)S(1)}, bf16[128,128]{1,0:T(8,128)(2,1)S(1)}, u32[]{:S(2)}, u32[]{:S(2)}) collective-permute-start(bf16[128,128]{1,0:T(8,128)(2,1)S(1)} %get-tuple-element.331), channel_id=1, source_target_pairs={{0,8},{8,16},{16,24},{24,32},{32,40},{40,48},{48,56},{56,64},{64,7... | collective-permute-start | bytes 98312 | tf_op jit(solution)/shard_map/while/body/eval_jaxpr/ppermute | solution.py:17
  194.0 10.1 %collective-permute-start.2 = (f32[128,128]{1,0:T(8,128)S(1)}, f32[128,128]{1,0:T(8,128)S(1)}, u32[]{:S(2)}, u32[]{:S(2)}) collective-permute-start(f32[128,128]{1,0:T(8,128)S(1)} %broadcast_select_fusion.2), channel_id=1, source_target_pairs={{0,8},{8,16},{16,24},{24,32},{32,40},{40,48},{48,56},{56,64},{64,7... | collective-permute-start | bytes 196616 | tf_op jit(solution)/shard_map/while/body/eval_jaxpr/ppermute | solution.py:17
  221.7 9.5 %collective-permute-start.2 = (f32[128,128]{1,0:T(8,128)S(1)}, f32[128,128]{1,0:T(8,128)S(1)}, u32[]{:S(2)}, u32[]{:S(2)}) collective-permute-start(f32[128,128]{1,0:T(8,128)S(1)} %broadcast_select_fusion.2), channel_id=1, source_target_pairs={{0,8},{8,16},{16,24},{24,32},{32,40},{40,48},{48,56},{56,64},{64,7... | collective-permute-start | bytes 196616 | tf_op jit(solution)/shard_map/while/body/eval_jaxpr/ppermute | solution.py:17
  235.3 9.4 %collective-permute-start.2 = (f32[128,128]{1,0:T(8,128)S(1)}, f32[128,128]{1,0:T(8,128)S(1)}, u32[]{:S(2)}, u32[]{:S(2)}) collective-permute-start(f32[128,128]{1,0:T(8,128)S(1)} %broadcast_select_fusion.2), channel_id=1, source_target_pairs={{0,8},{8,16},{16,24},{24,32},{32,40},{40,48},{48,56},{56,64},{64,7... | collective-permute-start | bytes 196616 | tf_op jit(solution)/shard_map/while/body/eval_jaxpr/ppermute | solution.py:17
  248.9 9.9 %collective-permute-start.2 = (f32[128,128]{1,0:T(8,128)S(1)}, f32[128,128]{1,0:T(8,128)S(1)}, u32[]{:S(2)}, u32[]{:S(2)}) collective-permute-start(f32[128,128]{1,0:T(8,128)S(1)} %broadcast_select_fusion.2), channel_id=1, source_target_pairs={{0,8},{8,16},{16,24},{24,32},{32,40},{40,48},{48,56},{56,64},{64,7... | collective-permute-start | bytes 196616 | tf_op jit(solution)/shard_map/while/body/eval_jaxpr/ppermute | solution.py:17
  276.5 9.6 %collective-permute-start.2 = (f32[128,128]{1,0:T(8,128)S(1)}, f32[128,128]{1,0:T(8,128)S(1)}, u32[]{:S(2)}, u32[]{:S(2)}) collective-permute-start(f32[128,128]{1,0:T(8,128)S(1)} %broadcast_select_fusion.2), channel_id=1, source_target_pairs={{0,8},{8,16},{16,24},{24,32},{32,40},{40,48},{48,56},{56,64},{64,7... | collective-permute-start | bytes 196616 | tf_op jit(solution)/shard_map/while/body/eval_jaxpr/ppermute | solution.py:17
  290.2 9.4 %collective-permute-start.2 = (f32[128,128]{1,0:T(8,128)S(1)}, f32[128,128]{1,0:T(8,128)S(1)}, u32[]{:S(2)}, u32[]{:S(2)}) collective-permute-start(f32[128,128]{1,0:T(8,128)S(1)} %broadcast_select_fusion.2), channel_id=1, source_target_pairs={{0,8},{8,16},{16,24},{24,32},{32,40},{40,48},{48,56},{56,64},{64,7... | collective-permute-start | bytes 196616 | tf_op jit(solution)/shard_map/while/body/eval_jaxpr/ppermute | solution.py:17
  354.1 9.5 %collective-permute-start = (bf16[128,128]{1,0:T(8,128)(2,1)S(1)}, bf16[128,128]{1,0:T(8,128)(2,1)S(1)}, u32[]{:S(2)}, u32[]{:S(2)}) collective-permute-start(bf16[128,128]{1,0:T(8,128)(2,1)S(1)} %get-tuple-element.330), channel_id=1, source_target_pairs={{0,8},{8,16},{16,24},{24,32},{32,40},{40,48},{48,56},{56,64},{64,7... | collective-permute-start | bytes 98312 | tf_op jit(solution)/shard_map/while/body/eval_jaxpr/ppermute | solution.py:17
  398.6 9.5 %collective-permute-start.2 = (f32[128,128]{1,0:T(8,128)S(1)}, f32[128,128]{1,0:T(8,128)S(1)}, u32[]{:S(2)}, u32[]{:S(2)}) collective-permute-start(f32[128,128]{1,0:T(8,128)S(1)} %broadcast_select_fusion.2), channel_id=1, source_target_pairs={{0,8},{8,16},{16,24},{24,32},{32,40},{40,48},{48,56},{56,64},{64,7... | collective-permute-start | bytes 196616 | tf_op jit(solution)/shard_map/while/body/eval_jaxpr/ppermute | solution.py:17
  412.2 9.4 %collective-permute-start.2 = (f32[128,128]{1,0:T(8,128)S(1)}, f32[128,128]{1,0:T(8,128)S(1)}, u32[]{:S(2)}, u32[]{:S(2)}) collective-permute-start(f32[128,128]{1,0:T(8,128)S(1)} %broadcast_select_fusion.2), channel_id=1, source_target_pairs={{0,8},{8,16},{16,24},{24,32},{32,40},{40,48},{48,56},{56,64},{64,7... | collective-permute-start | bytes 196616 | tf_op jit(solution)/shard_map/while/body/eval_jaxpr/ppermute | solution.py:17
  425.7 9.9 %collective-permute-start.2 = (f32[128,128]{1,0:T(8,128)S(1)}, f32[128,128]{1,0:T(8,128)S(1)}, u32[]{:S(2)}, u32[]{:S(2)}) collective-permute-start(f32[128,128]{1,0:T(8,128)S(1)} %broadcast_select_fusion.2), channel_id=1, source_target_pairs={{0,8},{8,16},{16,24},{24,32},{32,40},{40,48},{48,56},{56,64},{64,7... | collective-permute-start | bytes 196616 | tf_op jit(solution)/shard_map/while/body/eval_jaxpr/ppermute | solution.py:17
  453.3 9.6 %collective-permute-start.2 = (f32[128,128]{1,0:T(8,128)S(1)}, f32[128,128]{1,0:T(8,128)S(1)}, u32[]{:S(2)}, u32[]{:S(2)}) collective-permute-start(f32[128,128]{1,0:T(8,128)S(1)} %broadcast_select_fusion.2), channel_id=1, source_target_pairs={{0,8},{8,16},{16,24},{24,32},{32,40},{40,48},{48,56},{56,64},{64,7... | collective-permute-start | bytes 196616 | tf_op jit(solution)/shard_map/while/body/eval_jaxpr/ppermute | solution.py:17
  467.0 9.4 %collective-permute-start.2 = (f32[128,128]{1,0:T(8,128)S(1)}, f32[128,128]{1,0:T(8,128)S(1)}, u32[]{:S(2)}, u32[]{:S(2)}) collective-permute-start(f32[128,128]{1,0:T(8,128)S(1)} %broadcast_select_fusion.2), channel_id=1, source_target_pairs={{0,8},{8,16},{16,24},{24,32},{32,40},{40,48},{48,56},{56,64},{64,7... | collective-permute-start | bytes 196616 | tf_op jit(solution)/shard_map/while/body/eval_jaxpr/ppermute | solution.py:17
  476.7 54.4 %all-to-all-start = ((f32[8,128,128]{2,1,0:T(8,128)}), f32[8,128,128]{2,1,0:T(8,128)S(1)}, u32[]{:S(2)}, u32[]{:S(2)}) async-start(f32[8,128,128]{2,1,0:T(8,128)} %bitcast), calls=%async_computation | async-start | bytes 1048576 | tf_op jit(solution)/shard_map/all_to_all | solution.py:28
  515.9 288.4 %all-reduce.3.cloned.1.call-start = ((), (), s32[]{:S(2)}) async-start(), calls=%async_computation.1 | async-start | bytes 2097152 | tf_op jit(solution)/shard_map/psum | solution.py:92
  516.0 15.2 %collective-permute-start.3 = (f32[128,128]{0,1:T(8,128)S(1)}, f32[128,128]{0,1:T(8,128)S(1)}, u32[]{:S(2)}, u32[]{:S(2)}) collective-permute-start(f32[128,128]{0,1:T(8,128)S(1)} %copy.30), channel_id=1, source_target_pairs={{0,256},{8,264},{16,272},{24,280},{32,288},{40,296},{48,304},{56,3... | collective-permute-start | bytes 196616 | tf_op jit(solution)/shard_map/ppermute | solution.py:17
  (82 other events, 683.8 us)
Sparse Core Ops, SparseCore 0:
  534.0 270.2 all-reduce.2
where the time goes:
time: 819 us; the launch traced here: 814 us
  waiting for transfers between devices  337 us (41%)
  starting transfers between devices  229 us (28%)
  blocking collectives  119 us (15%)
  matrix products  99.2 us (12%)
  between operations  14.2 us (2%)
    ppermute x97, starting transfers between devices, from_behind(): return lax.ppermute(value, axis, pairs)  190 us
    psum x1, waiting for transfers between devices, local(): lax.psum((part_w_in, part_b_in, part_w_out), ('blk', 'row'))  172 us
    ppermute x97, waiting for transfers between devices, from_behind(): return lax.ppermute(value, axis, pairs)  153 us
    psum x1, blocking collectives, local(): lax.psum((part_w_in, part_b_in, part_w_out), ('blk', 'row'))  97.2 us
    dot_general x33, matrix products, tile(): lax.dot_general(weight_b, visit_g, down, preferred_element_type=jnp.float32)  68.8 us
    all_to_all x1, starting transfers between devices, sum_at_owner(): lax.all_to_all(blocks, axis, split_axis=0, concat_axis=0, tiled=True)  39.2 us
    all_gather x1, blocking collectives, sent_together(): result = lax.all_gather(both, axis, axis=dim, tiled=True)  21.6 us
  transfers between devices with their start and end apart: 99, of which 73 were waited for; matrix products, arithmetic and copies ran while one was open for 11% of the time, Pallas kernels for 0%

commit v1 on v0

v1 whole, which is shorter than its diff:
```python
import jax
import jax.numpy as jnp
from jax import lax
from jax.experimental import pallas as pl
from jax.experimental.pallas import tpu as pltpu
from jax.sharding import PartitionSpec as P

NX, NY, NZ, NC = 4, 8, 8, 2
PT = 128
PR = 144
D = 128
HID = 1024
HALF = 512
BF = jnp.bfloat16
F32 = jnp.float32
MESH = pl.DeviceIdType.MESH
NT = (((1,), (1,)), ((), ()))


def split3(v):
    hi = v.astype(BF)
    rest = v - hi.astype(F32)
    mid = rest.astype(BF)
    lo = (rest - mid.astype(F32)).astype(BF)
    return hi, mid, lo


def body(
    points, w_in, b_in, w_out, scales, left, right,
    fg_out, gi_out, gb_out, go_out,
    slope, hid_t, pts_t, rows, cols, rg, rb, ni, acc, sw, t_send, t_in,
    g, x_in, s1, in1, in2, in3, fin,
    send_y, recv_y, send_x, recv_x, send_z, recv_z, send_p, recv_p,
    send_t, recv_t, send_c, recv_c, send_1, recv_1, send_2, recv_2, send_3, recv_3, send_4, recv_4,
):
    blk = lax.axis_index("blk")
    row = lax.axis_index("row")
    y_lo = blk // (NX * NZ)
    z = (blk // NX) % NZ
    x = blk % NX
    c = row % 2
    y = (row // 2) * 2 + y_lo

    def dev(y_, z_, x_, c_):
        return (((y_ % 2) * NZ + z_) * NX + x_, (y_ // 2) * 2 + c_)

    def at_y(k):
        return dev(k, z, x, c)

    def at_z(k):
        return dev(y, k, x, c)

    def at_x(k):
        return dev(y, z, k, c)

    partner = dev(y, z, x, 1 - c)
    nxt = at_z((z + 1) % NZ)
    prv = at_z((z + NZ - 1) % NZ)

    def remote(src, dst, ss, rs, device):
        return pltpu.make_async_remote_copy(
            src_ref=src, dst_ref=dst, send_sem=ss, recv_sem=rs, device_id=device, device_id_type=MESH
        )

    bar = pltpu.get_barrier_semaphore()

    def hello(device):
        pl.semaphore_signal(bar, inc=1, device_id=device, device_id_type=MESH)

    hello(partner)
    for k in range(1, NX):
        hello(at_x((x + k) % NX))
    for k in range(1, NZ):
        hello(at_z((z + k) % NZ))
    for k in range(1, NY):
        hello(at_y((y + k) % NY))

    pts = points[...]
    pre = jnp.dot(pts, w_in[...], preferred_element_type=F32) + b_in[...]
    sig = jax.nn.sigmoid(pre)
    hidden = (pre * sig).astype(BF)
    feats = jnp.dot(hidden, w_out[...], preferred_element_type=F32)
    scaled = (feats * scales[...]).astype(BF)
    sf = scaled.astype(F32)
    sq = sf * sf
    sq_hi = sq.astype(BF)
    sq_lo = (sq - sq_hi.astype(F32)).astype(BF)
    ones = jnp.full((16, D), 0.5, BF)
    norm = lax.dot_general(ones, sq_hi, NT, preferred_element_type=F32) + lax.dot_general(
        ones, sq_lo, NT, preferred_element_type=F32
    )
    hi, mid, lo = split3(norm)
    which = lax.broadcasted_iota(jnp.int32, (16, D), 0)
    zero = jnp.zeros((16, D), F32)
    tail = jnp.where(
        which == 0, hi.astype(F32), jnp.where(which == 1, mid.astype(F32), jnp.where(which == 2, lo.astype(F32), zero))
    ).astype(BF)
    mine = cols.at[c, z, x]
    mine[0:PT, 0:D] = scaled
    mine[0:PT, D : D + 64] = left[...]
    mine[0:PT, D + 64 : 2 * D] = right[...]
    mine[PT:PR, 0:D] = tail
    mine[PT:PR, D : 2 * D] = jnp.zeros((16, D), BF)

    pl.semaphore_wait(bar, 1 + (NX - 1) + (NZ - 1) + (NY - 1))

    def slot_y(k):
        return jnp.where(k == 4, 7, jnp.where(k == 0, 0, jnp.where(k > 4, 2 * (8 - k) - 1, 2 * k)))

    def z_right(zz, xx):
        return remote(cols.at[c, zz, xx], cols.at[c, zz, xx], send_z.at[0, zz, xx], recv_z.at[zz, xx], nxt)

    def z_left(zz, xx):
        return remote(cols.at[c, zz, xx], cols.at[c, zz, xx], send_z.at[1, zz, xx], recv_z.at[zz, xx], prv)

    def to_partner(zz, xx):
        return remote(cols.at[c, zz, xx], cols.at[c, zz, xx], send_p.at[zz, xx], recv_p.at[zz, xx], partner)

    def from_partner(zz, xx):
        return remote(cols.at[1 - c, zz, xx], cols.at[1 - c, zz, xx], send_p.at[zz, xx], recv_p.at[zz, xx], partner)

    def x_copy(k):
        return remote(mine, mine, send_x.at[k], recv_x.at[x], at_x((x + k) % NX))

    def x_from(xx):
        return remote(mine, cols.at[c, z, xx], send_x.at[0], recv_x.at[xx], partner)

    def y_copy(k):
        return remote(mine, rows.at[slot_y((8 - k) % 8)], send_y.at[k], recv_y.at[slot_y((8 - k) % 8)], at_y((y + k) % NY))

    def y_from(s):
        return remote(mine, rows.at[s], send_y.at[0], recv_y.at[s], partner)

    z_right(z, x).start()
    z_left(z, x).start()
    for k in (1, 3, 2):
        x_copy(k).start()
    to_partner(z, x).start()
    for k in (1, 7, 2, 6, 3, 5, 4):
        y_copy(k).start()

    rows[0] = mine[...]
    slope[...] = sig * (1.0 + pre * (1.0 - sig))
    hid_t[...] = hidden.astype(F32).T.astype(BF)
    pts_t[...] = pts.astype(F32).T.astype(BF)

    for k in (1, 3, 2):
        xx = (x + k) % NX
        x_from(xx).wait_recv()
        z_right(z, xx).start()
        z_left(z, xx).start()
        to_partner(z, xx).start()

    acc[...] = jnp.zeros_like(acc)
    sw[...] = jnp.zeros_like(sw)

    def ready_rows(s):
        if s > 0:
            y_from(s).wait_recv()
        gg = rows[s, 0:PT, 0:D]
        ab = rows[s, 0:PT, D : 2 * D].astype(F32)
        at = pl.ds(s * PT, PT)
        rg[at, :] = gg
        rb[at, :] = pltpu.roll(ab, 64, 1).astype(BF)
        gf = gg.astype(F32)
        ni[at, :] = jnp.broadcast_to(0.5 * jnp.sum(gf * gf, axis=1, keepdims=True), (PT, D))

    for s in range(4):
        ready_rows(s)

    def unit(t):
        edge = jnp.logical_or(t == 0, t == 7)
        dist = (t + 1) // 2
        return edge, dist

    def block_of(t, way):
        edge, dist = unit(t)
        zz = jnp.where(way == 0, (z + NZ - dist) % NZ, (z + dist) % NZ)
        h = jnp.where(edge, way, (t + 1) % 2)
        return zz, h

    def arrivals(t):
        _, dist = unit(t)
        for way in (0, 1):
            zz, h = block_of(t, way)
            on = jnp.logical_or(dist + 1 < 4, jnp.logical_and(dist == 3, h == way))
            for i in (0, 1):
                xx = 2 * h + i
                hop = z_right(zz, xx) if way == 0 else z_left(zz, xx)
                hop.wait_recv()

                @pl.when(on)
                def _():
                    hop.start()

                to_partner(zz, xx).start()

    def tile(t, half):
        at = pl.ds(pl.multiple_of(half * HALF, HALF), HALF)

        def pair(q, carry):
            cc = (c + q // 2) % 2
            zz, h = block_of(t, q % 2)
            both = pl.ds(2 * h, 2)
            cg = cols[cc, zz, both, 0:PT, 0:D].reshape(2 * PT, D)
            cb = cols[cc, zz, both, 0:PT, D : 2 * D].reshape(2 * PT, D)
            nt = cols[cc, zz, both, PT:PR, 0:D].astype(F32)
            nj = jnp.concatenate([nt[0, 0:1] + nt[0, 1:2] + nt[0, 2:3], nt[1, 0:1] + nt[1, 1:2] + nt[1, 2:3]], axis=1)
            nh = ni[at, :]
            cross = lax.dot_general(rg[at, :], cg, NT, preferred_element_type=F32)
            coup = lax.dot_general(rb[at, :], cb, NT, preferred_element_type=F32)
            kern = jnp.exp(cross - jnp.concatenate([nh, nh], axis=1) - nj)
            weight = coup * kern
            sw[at, :] += weight[:, 0:D] + weight[:, D : 2 * D]
            acc[at, :] += jnp.dot(weight.astype(BF), cg, preferred_element_type=F32)
            return carry

        lax.fori_loop(0, 4, pair, 0)

    def partner_ready(t):
        for way in (0, 1):
            zz, h = block_of(t, way)
            for i in (0, 1):
                from_partner(zz, 2 * h + i).wait_recv()

    arrivals(1)
    partner_ready(0)
    tile(0, 0)
    arrivals(2)
    partner_ready(1)
    tile(1, 0)
    for s in range(4, 8):
        ready_rows(s)

    def main(j, carry):
        late = j - 2
        t = jnp.where(j < 2, j, 2 + late // 2)
        half = jnp.where(j < 2, 1, jnp.where(j >= 12, 1 - late % 2, late % 2))
        first = jnp.logical_and(j >= 2, late % 2 == 0)

        @pl.when(jnp.logical_and(first, t < 7))
        def _():
            arrivals(t + 1)

        @pl.when(first)
        def _():
            partner_ready(t)

        tile(t, half)
        return carry

    lax.fori_loop(0, 14, main, 0)

    def dist_of(s):
        return (0, 7, 1, 6, 2, 5, 3, 4)[s]

    def part(s):
        at = pl.ds(s * PT, PT)
        total = jnp.sum(sw[at, :], axis=1, keepdims=True)
        return acc[at, :] - total * rg[at, :].astype(F32)

    def t_copy(s):
        k = dist_of(s)
        there = (0, 2, 1, 4, 3, 6, 5, 7)[s]
        return remote(t_send.at[s], t_in.at[there], send_t.at[s], recv_t.at[there], at_y((y + k) % NY))

    for s in range(7, 0, -1):
        t_send[s] = part(s).astype(BF)
    for s in range(7, 0, -1):
        t_copy(s).start()
    total = part(0)
    for s in range(1, 8):
        remote(t_send.at[s], t_in.at[s], send_t.at[s], recv_t.at[s], partner).wait_recv()
        total += t_in[s].astype(F32)

    fg = total * scales[...]
    fg_out[...] = fg
    fgb = fg.astype(BF)
    part_out = jnp.dot(hid_t[...], fgb, preferred_element_type=F32).astype(BF)
    pg = lax.dot_general(fgb, w_out[...], NT, preferred_element_type=F32) * slope[...]
    pb = jnp.sum(pg, axis=0, keepdims=True)
    part_in = jnp.dot(pts_t[...], pg.astype(BF), preferred_element_type=F32).astype(BF)
    tilei = lax.broadcasted_iota(jnp.int32, (16, D), 0)

    def bias_tile(v):
        v_hi, v_mid, v_lo = split3(v)
        z16 = jnp.zeros((16, D), F32)
        return jnp.where(
            tilei == 0, v_hi.astype(F32), jnp.where(tilei == 1, v_mid.astype(F32), jnp.where(tilei == 2, v_lo.astype(F32), z16))
        ).astype(BF)

    for k in range(8):
        g[0, k, 0:PT, :] = part_out[k * PT : (k + 1) * PT, :]
        g[0, k, PT:PR, :] = jnp.zeros((16, D), BF)
        g[1, k, 0:PT, :] = part_in[:, k * D : (k + 1) * D]
        g[1, k, PT:PR, :] = bias_tile(jnp.broadcast_to(pb[:, k * D : (k + 1) * D], (16, D)))

    def at_1(k):
        return dev(jnp.where(c == 0, y, k), jnp.where(c == 0, k, z), x, c)

    def at_2(k):
        return dev(jnp.where(c == 0, k, y), jnp.where(c == 0, z, k), x, c)

    me1 = jnp.where(c == 0, z, y)
    me2 = jnp.where(c == 0, y, z)

    def packed(v):
        b = jnp.sum(v[PT : PT + 8], axis=0, keepdims=True)
        return v[0:PT].astype(BF), bias_tile(jnp.broadcast_to(b, (16, D)))

    half_copy = remote(g.at[1 - c], x_in, send_c.at[0], recv_c.at[0], partner)
    half_copy.start()
    half_copy.wait_recv()

    def combine(k, carry):
        a, b = packed(g[c, k].astype(F32) + x_in[k].astype(F32))
        s1[k, 0:PT] = a
        s1[k, PT:PR] = b
        return carry

    lax.fori_loop(0, 8, combine, 0)

    def line(peers, me, n, src_of, slots, ss, rs):
        def go(k, carry):
            to = (me + k) % n
            remote(src_of(to), slots.at[me], ss.at[k], rs.at[me], peers(to)).start()
            return carry

        def come(k, carry):
            at = (me + k) % n
            remote(src_of(at), slots.at[at], ss.at[k], rs.at[at], peers(at)).wait_recv()
            return carry

        def sent(k, carry):
            to = (me + k) % n
            remote(src_of(to), slots.at[me], ss.at[k], rs.at[me], peers(to)).wait_send()
            return carry

        lax.fori_loop(1, n, go, 0)
        return lambda: lax.fori_loop(1, n, come, 0), lambda: lax.fori_loop(1, n, sent, 0)

    come, sent1 = line(at_1, me1, 8, lambda k: s1.at[k], in1, send_1, recv_1)
    in1[me1] = s1[me1]
    come()
    tot = in1[0].astype(F32)
    for k in range(1, 8):
        tot += in1[k].astype(F32)
    a, b = packed(tot)
    in2[me2, 0:PT] = a
    in2[me2, PT:PR] = b
    come, sent2 = line(at_2, me2, 8, lambda k: in2.at[me2], in2, send_2, recv_2)
    come()
    tot = in2[0].astype(F32)
    for k in range(1, 8):
        tot += in2[k].astype(F32)
    a, b = packed(tot)
    in3[x, 0:PT] = a
    in3[x, PT:PR] = b
    come, sent3 = line(at_x, x, NX, lambda k: in3.at[x], in3, send_3, recv_3)
    come()
    tot = in3[0].astype(F32)
    for k in range(1, NX):
        tot += in3[k].astype(F32)
    a, b = packed(tot)
    fin[c, me1, 0:PT] = a
    fin[c, me1, PT:PR] = b
    come, sent4 = line(at_1, me1, 8, lambda k: fin.at[c, me1], fin.at[c], send_4, recv_4)
    come()
    out_copy = remote(fin.at[c], fin.at[c], send_c.at[1], recv_c.at[1], partner)
    out_copy.start()
    remote(fin.at[1 - c], fin.at[1 - c], send_c.at[1], recv_c.at[1], partner).wait_recv()

    factor = 1.0 / 256.0
    for k in range(8):
        go_out[k * PT : (k + 1) * PT, :] = factor * fin[0, k, 0:PT].astype(F32)
        gi_out[:, k * D : (k + 1) * D] = factor * fin[1, k, 0:PT].astype(F32)
        bt = fin[1, k, PT:PR].astype(F32)
        gb_out[k : k + 1, :] = factor * (bt[0:1] + bt[1:2] + bt[2:3])

    for k in (1, 3, 2):
        x_copy(k).wait_send()
    for k in range(1, 8):
        y_copy(k).wait_send()
        t_copy(k).wait_send()

    def z_sent(i, carry):
        zz, xx = i // NX, i % NX
        back = (z + NZ - zz) % NZ
        ahead = (zz + NZ - z) % NZ

        @pl.when(jnp.logical_or(back < 3, jnp.logical_and(back == 3, xx < 2)))
        def _():
            z_right(zz, xx).wait_send()

        @pl.when(jnp.logical_or(ahead < 3, jnp.logical_and(ahead == 3, xx >= 2)))
        def _():
            z_left(zz, xx).wait_send()

        to_partner(zz, xx).wait_send()
        return carry

    lax.fori_loop(0, NZ * NX, z_sent, 0)
    half_copy.wait_send()
    out_copy.wait_send()
    sent1()
    sent2()
    sent3()
    sent4()


def local(points, w_in, b_in, w_out, scales, left, right):
    vmem = pl.BlockSpec(memory_space=pltpu.VMEM)
    dma = pltpu.SemaphoreType.DMA
    piece = (PR, D)
    fg, gi, gb, go = pl.pallas_call(
        body,
        out_shape=[
            jax.ShapeDtypeStruct((PT, D), F32),
            jax.ShapeDtypeStruct((D, HID), F32),
            jax.ShapeDtypeStruct((8, D), F32),
            jax.ShapeDtypeStruct((HID, D), F32),
        ],
        in_specs=[vmem] * 7,
        out_specs=[vmem] * 4,
        scratch_shapes=[
            pltpu.VMEM((PT, HID), F32),
            pltpu.VMEM((HID, PT), BF),
            pltpu.VMEM((D, PT), BF),
            pltpu.VMEM((NY, PR, 2 * D), BF),
            pltpu.VMEM((NC, NZ, NX, PR, 2 * D), BF),
            pltpu.VMEM((NY * PT, D), BF),
            pltpu.VMEM((NY * PT, D), BF),
            pltpu.VMEM((NY * PT, D), F32),
            pltpu.VMEM((NY * PT, D), F32),
            pltpu.VMEM((NY * PT, D), F32),
            pltpu.VMEM((NY, PT, D), BF),
            pltpu.VMEM((NY, PT, D), BF),
            pltpu.VMEM((2, 8) + piece, BF),
            pltpu.VMEM((8,) + piece, BF),
            pltpu.VMEM((8,) + piece, BF),
            pltpu.VMEM((8,) + piece, BF),
            pltpu.VMEM((8,) + piece, BF),
            pltpu.VMEM((NX,) + piece, BF),
            pltpu.VMEM((2, 8) + piece, BF),
            dma((8,)), dma((8,)), dma((4,)), dma((4,)),
            dma((2, NZ, NX)), dma((NZ, NX)), dma((NZ, NX)), dma((NZ, NX)),
            dma((8,)), dma((8,)), dma((2,)), dma((2,)),
            dma((8,)), dma((8,)), dma((8,)), dma((8,)), dma((4,)), dma((4,)), dma((8,)), dma((8,)),
        ],
        compiler_params=pltpu.CompilerParams(collective_id=0, has_side_effects=True),
        name="gp_grad",
    )(points, w_in, b_in.reshape(1, HID), w_out, scales.reshape(1, D), left, right)
    return fg, gi, gb.reshape(HID), go


def solution(mesh):
    placed = (
        P(("blk", "row"), None),
        P(),
        P(),
        P(),
        P(),
        P(("blk", "row"), None),
        P(("blk", "row"), None),
    )
    return jax.shard_map(
        local,
        mesh=mesh,
        in_specs=placed,
        out_specs=(P(("blk", "row"), None), P(), P(), P()),
        check_vma=False,
    )
```

time: 819 us -> 107 us (0.13)
  waiting for transfers between devices: 337 us -> 0 us
  starting transfers between devices: 229 us -> 0 us
  blocking collectives: 119 us -> 0 us
  Pallas kernels: 0 us -> 99.6 us
  matrix products: 99.2 us -> 0 us
  between operations: 14.2 us -> 0.65 us
    ppermute x97 -> x0, starting transfers between devices: 190 us -> none  [from_behind(): return lax.ppermute(value, axis, pairs)]
    psum x1 -> x0, waiting for transfers between devices: 172 us -> none  [local(): lax.psum((part_w_in, part_b_in, part_w_out), ('blk', 'row'))]
    ppermute x97 -> x0, waiting for transfers between devices: 153 us -> none  [from_behind(): return lax.ppermute(value, axis, pairs)]
    pallas_call x0 -> x1, Pallas kernels: none -> 99.6 us  [local(): pl.pallas_call(body, out_shape=[jax.ShapeDtypeStruct((PT, D), F32), jax.S...]
    dot_general x136 -> x0, matrix products: 99.2 us -> none  [the longest x33 68.8 us: tile(): lax.dot_general(weight_b, visit_g, down, preferred_element_type=jnp.float32)]
    psum x1 -> x0, blocking collectives: 97.2 us -> none  [local(): lax.psum((part_w_in, part_b_in, part_w_out), ('blk', 'row'))]
    all_to_all x1 -> x0, starting transfers between devices: 39.2 us -> none  [sum_at_owner(): lax.all_to_all(blocks, axis, split_axis=0, concat_axis=0, tiled=True)]
    all_gather x1 -> x0, blocking collectives: 21.6 us -> none  [sent_together(): result = lax.all_gather(both, axis, axis=dim, tiled=True)]
  transfers between devices with their start and end apart: 99 -> 0, of which waited for: 73 -> 0; matrix products, arithmetic and copies ran while one was open for 11% -> 0% of each run, Pallas kernels for 0% -> 0%
where the time goes in v1:
time: 107 us
  Pallas kernels  99.6 us (93%)
  local copies, waits for them, and re-layouts  6.98 us (7%)
    pallas_call x1, Pallas kernels, local(): pl.pallas_call(body, out_shape=[jax.ShapeDtypeStruct((PT, D), F32), jax.S...  99.6 us
    unnamed x12, local copies, waits for them, and re-layouts  6.98 us

profile of v1, /device:TPU:1, one launch (start us, length us, event | category | flops | bytes accessed | tf_op | source)
XLA Modules:
  0.0 107.2 jit_solution(14983108175236515044)
XLA Ops:
  0.6 0.0 copy-start.1
  0.6 1.4 %copy.11.left = bf16[128,64]{1,0:T(8,128)(2,1)} copy(bf16[128,64]{0,1:T(8,128)(2,1)} %param.12) | data formatting | bytes 32768 | tf_op args[5]
  2.1 0.0 copy-done.1
  2.1 0.7 copy.12.right
  2.8 99.6 %gp_grad.1 = (f32[128,128]{1,0:T(8,128)}, f32[128,1024]{1,0:T(8,128)}, f32[8,128]{1,0:T(8,128)}, f32[1024,128]{1,0:T(8,128)}) custom-call(bf16[128,128]{1,0:T(8,128)(2,1)} %points.1, bf16[128,1024]{1,0:T(8,128)(2,1)} %w_in.1, f32[1,1024]{1,0:T(1,128)} %bitcast.3, bf16[1024,128]{1,0:T(8,128)(2,1)} %w_out.1, f32[1,128]{1,0:T(1,128)} %bitcast.5, ...), custom_call_target="tpu_custom_call" | custom-call | tf_op jit(solution)/shard_map/gp_grad/pallas_call | solution.py:415
  102.4 1.5 %copy.17 = f32[128,128]{1,0:T(8,128)} copy(f32[128,128]{1,0:T(8,128)} %get-tuple-element.16) | data formatting | bytes 131072
  103.9 0.0 copy-start.2
  103.9 0.0 copy-start
  103.9 1.9 %copy.18 = f32[128,1024]{1,0:T(8,128)} copy(f32[128,1024]{1,0:T(8,128)} %get-tuple-element.17) | data formatting | bytes 1048576
  105.8 0.0 copy-done.2
  105.8 0.6 copy.19
  106.4 0.0 copy-done
  106.4 0.8 copy.20
Async XLA Ops:
  0.6 1.5 %copy-start.1 = (bf16[128,64]{0,1:T(8,128)(2,1)S(1)}, bf16[128,64]{0,1:T(8,128)(2,1)}, u32[]{:S(2)}) copy-start(bf16[128,64]{0,1:T(8,128)(2,1)} %param.13) | copy-start | bytes 49156
  103.9 1.9 %copy-start.2 = (f32[8,128]{1,0:T(8,128)S(1)}, f32[8,128]{1,0:T(8,128)}, u32[]{:S(2)}) copy-start(f32[8,128]{1,0:T(8,128)} %get-tuple-element.10) | copy-start | bytes 12292
  103.9 2.5 %copy-start = (f32[1024,128]{1,0:T(8,128)S(1)}, f32[1024,128]{1,0:T(8,128)}, u32[]{:S(2)}) copy-start(f32[1024,128]{1,0:T(8,128)} %get-tuple-element.19) | copy-start | bytes 1572868

commit v2 on v1

--- a/solution.py
+++ b/solution.py
@@ -27,10 +27,10 @@
 
 def body(
     points, w_in, b_in, w_out, scales, left, right,
-    fg_out, gi_out, gb_out, go_out,
+    fg_out, fin_out,
     slope, hid_t, pts_t, rows, cols, rg, rb, ni, acc, sw, t_send, t_in,
     g, x_in, s1, in1, in2, in3, fin,
-    send_y, recv_y, send_x, recv_x, send_z, recv_z, send_p, recv_p,
+    send_y, recv_y, send_x, send_z, recv_a, send_p, recv_p,
     send_t, recv_t, send_c, recv_c, send_1, recv_1, send_2, recv_2, send_3, recv_3, send_4, recv_4,
 ):
     blk = lax.axis_index("blk")
@@ -97,8 +97,7 @@
     ).astype(BF)
     mine = cols.at[c, z, x]
     mine[0:PT, 0:D] = scaled
-    mine[0:PT, D : D + 64] = left[...]
-    mine[0:PT, D + 64 : 2 * D] = right[...]
+    mine[0:PT, D : 2 * D] = jnp.concatenate([left[...].astype(F32), right[...].astype(F32)], axis=0).T.astype(BF)
     mine[PT:PR, 0:D] = tail
     mine[PT:PR, D : 2 * D] = jnp.zeros((16, D), BF)
 
@@ -107,52 +106,83 @@
     def slot_y(k):
         return jnp.where(k == 4, 7, jnp.where(k == 0, 0, jnp.where(k > 4, 2 * (8 - k) - 1, 2 * k)))
 
+    def piece(zz, xx):
+        return cols.at[c, zz, xx]
+
+    def arrival(zz, xx):
+        return remote(piece(zz, xx), piece(zz, xx), send_p.at[zz, xx], recv_a.at[zz, xx], partner)
+
     def z_right(zz, xx):
-        return remote(cols.at[c, zz, xx], cols.at[c, zz, xx], send_z.at[0, zz, xx], recv_z.at[zz, xx], nxt)
+        return remote(piece(zz, xx), piece(zz, xx), send_z.at[0, zz, xx], recv_a.at[zz, xx], nxt)
 
     def z_left(zz, xx):
-        return remote(cols.at[c, zz, xx], cols.at[c, zz, xx], send_z.at[1, zz, xx], recv_z.at[zz, xx], prv)
+        return remote(piece(zz, xx), piece(zz, xx), send_z.at[1, zz, xx], recv_a.at[zz, xx], prv)
+
+    def z_direct(k):
+        return remote(mine, mine, send_z.at[0, k, 0], recv_a.at[z, x], at_z((z + k) % NZ))
+
+    def x_copy(zz, k):
+        return remote(piece(zz, x), piece(zz, x), send_x.at[zz, k], recv_a.at[zz, x], at_x((x + k) % NX))
 
     def to_partner(zz, xx):
-        return remote(cols.at[c, zz, xx], cols.at[c, zz, xx], send_p.at[zz, xx], recv_p.at[zz, xx], partner)
+        return remote(piece(zz, xx), piece(zz, xx), send_p.at[zz, xx], recv_p.at[zz, xx], partner)
 
     def from_partner(zz, xx):
         return remote(cols.at[1 - c, zz, xx], cols.at[1 - c, zz, xx], send_p.at[zz, xx], recv_p.at[zz, xx], partner)
 
-    def x_copy(k):
-        return remote(mine, mine, send_x.at[k], recv_x.at[x], at_x((x + k) % NX))
-
-    def x_from(xx):
-        return remote(mine, cols.at[c, z, xx], send_x.at[0], recv_x.at[xx], partner)
-
     def y_copy(k):
         return remote(mine, rows.at[slot_y((8 - k) % 8)], send_y.at[k], recv_y.at[slot_y((8 - k) % 8)], at_y((y + k) % NY))
 
     def y_from(s):
         return remote(mine, rows.at[s], send_y.at[0], recv_y.at[s], partner)
 
-    z_right(z, x).start()
-    z_left(z, x).start()
+    @pl.when(c == 0)
+    def _():
+        z_right(z, x).start()
+        z_left(z, x).start()
+
     for k in (1, 3, 2):
-        x_copy(k).start()
+        x_copy(z, k).start()
     to_partner(z, x).start()
-    for k in (1, 7, 2, 6, 3, 5, 4):
+    for k in (1, 7, 2, 6):
         y_copy(k).start()
+
+    @pl.when(c == 1)
+    def _():
+        for k in (1, 7, 2, 6, 3, 5, 4):
+            z_direct(k).start()
 
     rows[0] = mine[...]
     slope[...] = sig * (1.0 + pre * (1.0 - sig))
     hid_t[...] = hidden.astype(F32).T.astype(BF)
     pts_t[...] = pts.astype(F32).T.astype(BF)
+    acc[...] = jnp.zeros_like(acc)
+    sw[...] = jnp.zeros_like(sw)
 
     for k in (1, 3, 2):
         xx = (x + k) % NX
-        x_from(xx).wait_recv()
-        z_right(z, xx).start()
-        z_left(z, xx).start()
+        arrival(z, xx).wait_recv()
+
+        @pl.when(c == 0)
+        def _():
+            z_right(z, xx).start()
+            z_left(z, xx).start()
+
         to_partner(z, xx).start()
 
-    acc[...] = jnp.zeros_like(acc)
-    sw[...] = jnp.zeros_like(sw)
+    for k in (3, 5, 4):
+        y_copy(k).start()
+
+    def spread(zz):
+        arrival(zz, x).wait_recv()
+        for k in (1, 3, 2):
+            x_copy(zz, k).start()
+        to_partner(zz, x).start()
+
+    @pl.when(c == 1)
+    def _():
+        spread((z + NZ - 1) % NZ)
+        spread((z + 1) % NZ)
 
     def ready_rows(s):
         if s > 0:
@@ -168,54 +198,81 @@
     for s in range(4):
         ready_rows(s)
 
-    def unit(t):
+    def block_of(t, way):
         edge = jnp.logical_or(t == 0, t == 7)
         dist = (t + 1) // 2
-        return edge, dist
-
-    def block_of(t, way):
-        edge, dist = unit(t)
         zz = jnp.where(way == 0, (z + NZ - dist) % NZ, (z + dist) % NZ)
         h = jnp.where(edge, way, (t + 1) % 2)
         return zz, h
 
     def arrivals(t):
-        _, dist = unit(t)
-        for way in (0, 1):
-            zz, h = block_of(t, way)
-            on = jnp.logical_or(dist + 1 < 4, jnp.logical_and(dist == 3, h == way))
-            for i in (0, 1):
-                xx = 2 * h + i
-                hop = z_right(zz, xx) if way == 0 else z_left(zz, xx)
-                hop.wait_recv()
-
-                @pl.when(on)
-                def _():
-                    hop.start()
-
-                to_partner(zz, xx).start()
+        dist = (t + 1) // 2
+
+        @pl.when(c == 0)
+        def _():
+            for way in (0, 1):
+                zz, h = block_of(t, way)
+                on = jnp.logical_or(dist + 1 < 4, jnp.logical_and(dist == 3, h == way))
+                for i in (0, 1):
+                    xx = 2 * h + i
+                    arrival(zz, xx).wait_recv()
+
+                    @pl.when(on)
+                    def _():
+                        if way == 0:
+                            z_right(zz, xx).start()
+                        else:
+                            z_left(zz, xx).start()
+
+                    to_partner(zz, xx).start()
+
+        @pl.when(c == 1)
+        def _():
+            @pl.when(t < 4)
+            def _():
+                spread((z + NZ - (t + 1)) % NZ)
+
+            @pl.when(t < 3)
+            def _():
+                spread((z + t + 1) % NZ)
+
+            for way in (0, 1):
+                zz, h = block_of(t, way)
+                for i in (0, 1):
+                    xx = 2 * h + i
+
+                    @pl.when(xx != x)
+                    def _():
+                        arrival(zz, xx).wait_recv()
+                        to_partner(zz, xx).start()
 
     def tile(t, half):
         at = pl.ds(pl.multiple_of(half * HALF, HALF), HALF)
-
-        def pair(q, carry):
-            cc = (c + q // 2) % 2
-            zz, h = block_of(t, q % 2)
-            both = pl.ds(2 * h, 2)
-            cg = cols[cc, zz, both, 0:PT, 0:D].reshape(2 * PT, D)
-            cb = cols[cc, zz, both, 0:PT, D : 2 * D].reshape(2 * PT, D)
-            nt = cols[cc, zz, both, PT:PR, 0:D].astype(F32)
-            nj = jnp.concatenate([nt[0, 0:1] + nt[0, 1:2] + nt[0, 2:3], nt[1, 0:1] + nt[1, 1:2] + nt[1, 2:3]], axis=1)
-            nh = ni[at, :]
-            cross = lax.dot_general(rg[at, :], cg, NT, preferred_element_type=F32)
-            coup = lax.dot_general(rb[at, :], cb, NT, preferred_element_type=F32)
-            kern = jnp.exp(cross - jnp.concatenate([nh, nh], axis=1) - nj)
-            weight = coup * kern
-            sw[at, :] += weight[:, 0:D] + weight[:, D : 2 * D]
-            acc[at, :] += jnp.dot(weight.astype(BF), cg, preferred_element_type=F32)
+        nh = ni[at, :]
+        nh2 = jnp.concatenate([nh, nh], axis=1)
+
+        def quad(q, carry):
+            cc = (c + q) % 2
+            weights, gs = [], []
+            for way in (0, 1):
+                zz, h = block_of(t, way)
+                both = pl.ds(2 * h, 2)
+                cg = cols[cc, zz, both, 0:PT, 0:D].reshape(2 * PT, D)
+                cb = cols[cc, zz, both, 0:PT, D : 2 * D].reshape(2 * PT, D)
+                nt = cols[cc, zz, both, PT:PR, 0:D].astype(F32)
+                nj = jnp.concatenate([nt[0, 0:1] + nt[0, 1:2] + nt[0, 2:3], nt[1, 0:1] + nt[1, 1:2] + nt[1, 2:3]], axis=1)
+                cross = lax.dot_general(rg[at, :], cg, NT, preferred_element_type=F32)
+                coup = lax.dot_general(rb[at, :], cb, NT, preferred_element_type=F32)
+                weights.append(coup * jnp.exp(cross - nh2 - nj))
+                gs.append(cg)
+            v, w = weights
+            sw[at, :] += (v[:, 0:D] + v[:, D : 2 * D]) + (w[:, 0:D] + w[:, D : 2 * D])
+            acc[at, :] += jnp.dot(
+                jnp.concatenate([v.astype(BF), w.astype(BF)], axis=1), jnp.concatenate(gs, axis=0), preferred_element_type=F32
+            )
             return carry
 
-        lax.fori_loop(0, 4, pair, 0)
+        lax.fori_loop(0, 2, quad, 0, unroll=2)
 
     def partner_ready(t):
         for way in (0, 1):
@@ -223,34 +280,6 @@
             for i in (0, 1):
                 from_partner(zz, 2 * h + i).wait_recv()
 
-    arrivals(1)
-    partner_ready(0)
-    tile(0, 0)
-    arrivals(2)
-    partner_ready(1)
-    tile(1, 0)
-    for s in range(4, 8):
-        ready_rows(s)
-
-    def main(j, carry):
-        late = j - 2
-        t = jnp.where(j < 2, j, 2 + late // 2)
-        half = jnp.where(j < 2, 1, jnp.where(j >= 12, 1 - late % 2, late % 2))
-        first = jnp.logical_and(j >= 2, late % 2 == 0)
-
-        @pl.when(jnp.logical_and(first, t < 7))
-        def _():
-            arrivals(t + 1)
-
-        @pl.when(first)
-        def _():
-            partner_ready(t)
-
-        tile(t, half)
-        return carry
-
-    lax.fori_loop(0, 14, main, 0)
-
     def dist_of(s):
         return (0, 7, 1, 6, 2, 5, 3, 4)[s]
 
@@ -264,9 +293,42 @@
         there = (0, 2, 1, 4, 3, 6, 5, 7)[s]
         return remote(t_send.at[s], t_in.at[there], send_t.at[s], recv_t.at[there], at_y((y + k) % NY))
 
-    for s in range(7, 0, -1):
+    def main(j, carry):
+        t = jnp.where(j < 3, j, jnp.where(j < 6, j - 3, jnp.where(j < 12, 3 + (j - 6) // 2, 6 + (j - 12) % 2)))
+        half = jnp.where(j < 3, 0, jnp.where(j < 6, 1, jnp.where(j < 12, j % 2, 1 - (j - 12) // 2)))
+        even = j % 2 == 0
+        first = jnp.logical_or(j < 3, jnp.logical_or(jnp.logical_and(jnp.logical_and(j >= 6, j < 12), even), jnp.logical_or(j == 12, j == 13)))
+
+        @pl.when(j == 3)
+        def _():
+            for s in range(4, 8):
+                ready_rows(s)
+
+        @pl.when(j == 14)
+        def _():
+            for s in (7, 6, 5, 4):
+                t_send[s] = part(s).astype(BF)
+            for s in (7, 6, 5, 4):
+                t_copy(s).start()
+
+        @pl.when(first)
+        def _():
+            partner_ready(t)
+
+        tile(t, half)
+        later = jnp.logical_and(even, jnp.logical_and(j >= 4, j <= 10))
+
+        @pl.when(jnp.logical_or(j < 3, later))
+        def _():
+            arrivals(jnp.where(j < 3, j + 1, j // 2 + 2))
+
+        return carry
+
+    lax.fori_loop(0, 16, main, 0)
+
+    for s in (3, 2, 1):
         t_send[s] = part(s).astype(BF)
-    for s in range(7, 0, -1):
+    for s in (3, 2, 1):
         t_copy(s).start()
     total = part(0)
     for s in range(1, 8):
@@ -370,36 +432,41 @@
     out_copy.start()
     remote(fin.at[1 - c], fin.at[1 - c], send_c.at[1], recv_c.at[1], partner).wait_recv()
 
-    factor = 1.0 / 256.0
-    for k in range(8):
-        go_out[k * PT : (k + 1) * PT, :] = factor * fin[0, k, 0:PT].astype(F32)
-        gi_out[:, k * D : (k + 1) * D] = factor * fin[1, k, 0:PT].astype(F32)
-        bt = fin[1, k, PT:PR].astype(F32)
-        gb_out[k : k + 1, :] = factor * (bt[0:1] + bt[1:2] + bt[2:3])
+    fin_out[...] = fin[...]
 
     for k in (1, 3, 2):
-        x_copy(k).wait_send()
+        x_copy(z, k).wait_send()
     for k in range(1, 8):
         y_copy(k).wait_send()
         t_copy(k).wait_send()
 
-    def z_sent(i, carry):
+    def sent(i, carry):
         zz, xx = i // NX, i % NX
         back = (z + NZ - zz) % NZ
         ahead = (zz + NZ - z) % NZ
 
-        @pl.when(jnp.logical_or(back < 3, jnp.logical_and(back == 3, xx < 2)))
-        def _():
-            z_right(zz, xx).wait_send()
-
-        @pl.when(jnp.logical_or(ahead < 3, jnp.logical_and(ahead == 3, xx >= 2)))
-        def _():
-            z_left(zz, xx).wait_send()
+        @pl.when(c == 0)
+        def _():
+            @pl.when(jnp.logical_or(back < 3, jnp.logical_and(back == 3, xx < 2)))
+            def _():
+                z_right(zz, xx).wait_send()
+
+            @pl.when(jnp.logical_or(ahead < 3, jnp.logical_and(ahead == 3, xx >= 2)))
+            def _():
+                z_left(zz, xx).wait_send()
 
         to_partner(zz, xx).wait_send()
         return carry
 
-    lax.fori_loop(0, NZ * NX, z_sent, 0)
+    lax.fori_loop(0, NZ * NX, sent, 0)
+
+    @pl.when(c == 1)
+    def _():
+        for k in range(1, NZ):
+            z_direct(k).wait_send()
+            for m in (1, 3, 2):
+                x_copy((z + k) % NZ, m).wait_send()
+
     half_copy.wait_send()
     out_copy.wait_send()
     sent1()
@@ -408,20 +475,28 @@
     sent4()
 
 
+def finish(fg_in, fin, fg_out, gi_out, gb_out, go_out):
+    factor = 1.0 / 256.0
+    fg_out[...] = fg_in[...]
+    for k in range(8):
+        go_out[k * PT : (k + 1) * PT, :] = factor * fin[0, k, 0:PT].astype(F32)
+        gi_out[:, k * D : (k + 1) * D] = factor * fin[1, k, 0:PT].astype(F32)
+        bt = fin[1, k, PT:PR].astype(F32)
+        gb_out[k : k + 1, :] = factor * (bt[0:1] + bt[1:2] + bt[2:3])
+
+
 def local(points, w_in, b_in, w_out, scales, left, right):
     vmem = pl.BlockSpec(memory_space=pltpu.VMEM)
     dma = pltpu.SemaphoreType.DMA
     piece = (PR, D)
-    fg, gi, gb, go = pl.pallas_call(
+    fg, sums = pl.pallas_call(
         body,
         out_shape=[
             jax.ShapeDtypeStruct((PT, D), F32),
-            jax.ShapeDtypeStruct((D, HID), F32),
-            jax.ShapeDtypeStruct((8, D), F32),
-            jax.ShapeDtypeStruct((HID, D), F32),
+            jax.ShapeDtypeStruct((2, 8) + piece, BF),
         ],
         in_specs=[vmem] * 7,
-        out_specs=[vmem] * 4,
+        out_specs=[vmem] * 2,
         scratch_shapes=[
             pltpu.VMEM((PT, HID), F32),
             pltpu.VMEM((HID, PT), BF),
@@ -442,14 +517,26 @@
             pltpu.VMEM((8,) + piece, BF),
             pltpu.VMEM((NX,) + piece, BF),
             pltpu.VMEM((2, 8) + piece, BF),
-            dma((8,)), dma((8,)), dma((4,)), dma((4,)),
+            dma((8,)), dma((8,)), dma((NZ, NX)),
             dma((2, NZ, NX)), dma((NZ, NX)), dma((NZ, NX)), dma((NZ, NX)),
             dma((8,)), dma((8,)), dma((2,)), dma((2,)),
             dma((8,)), dma((8,)), dma((8,)), dma((8,)), dma((4,)), dma((4,)), dma((8,)), dma((8,)),
         ],
         compiler_params=pltpu.CompilerParams(collective_id=0, has_side_effects=True),
         name="gp_grad",
-    )(points, w_in, b_in.reshape(1, HID), w_out, scales.reshape(1, D), left, right)
+    )(points, w_in, b_in.reshape(1, HID), w_out, scales.reshape(1, D), left.T, right.T)
+    fg, gi, gb, go = pl.pallas_call(
+        finish,
+        out_shape=[
+            jax.ShapeDtypeStruct((PT, D), F32),
+            jax.ShapeDtypeStruct((D, HID), F32),
+            jax.ShapeDtypeStruct((8, D), F32),
+            jax.ShapeDtypeStruct((HID, D), F32),
+        ],
+        in_specs=[vmem] * 2,
+        out_specs=[vmem] * 4,
+        name="finish",
+    )(fg, sums)
     return fg, gi, gb.reshape(HID), go
 
 

time: 107 us -> 90.3 us (0.84)
  Pallas kernels: 99.6 us -> 89.5 us
  local copies, waits for them, and re-layouts: 6.98 us -> 0 us
    pallas_call x1, Pallas kernels: 99.6 us -> 87.4 us  [local(): pl.pallas_call(body, out_shape=[jax.ShapeDtypeStruct((PT, D), F32), jax.S...]
    unnamed x12 -> x0, local copies, waits for them, and re-layouts: 6.98 us -> none
    pallas_call x0 -> x1, Pallas kernels: none -> 2.13 us  [local(): pl.pallas_call(finish, out_shape=[jax.ShapeDtypeStruct((PT, D), F32), jax...]
where the time goes in v2:
time: 90.3 us; the launch traced here: 90.2 us
  Pallas kernels  89.5 us (99%)
    pallas_call x1, Pallas kernels, local(): pl.pallas_call(body, out_shape=[jax.ShapeDtypeStruct((PT, D), F32), jax.S...  87.4 us
    pallas_call x1, Pallas kernels, local(): pl.pallas_call(finish, out_shape=[jax.ShapeDtypeStruct((PT, D), F32), jax...  2.13 us

profile of v2, /device:TPU:1, one launch (start us, length us, event | category | flops | bytes accessed | tf_op | source)
XLA Modules:
  0.0 90.2 jit_solution(13834603890302736707)
XLA Ops:
  0.6 87.4 %gp_grad.1 = (f32[128,128]{1,0:T(8,128)}, bf16[2,8,144,128]{3,2,1,0:T(8,128)(2,1)}) custom-call(bf16[128,128]{1,0:T(8,128)(2,1)} %points.1, bf16[128,1024]{1,0:T(8,128)(2,1)} %w_in.1, f32[1,1024]{1,0:T(1,128)} %bitcast.7, bf16[1024,128]{1,0:T(8,128)(2,1)} %w_out.1, f32[1,128]{1,0:T(1,128)} %bitcast.8, bf16[64,128]{1,0:T(8,128)(2,1)} %bitcast.5, ...), custom_call_target="tpu_custom_call" | custom-call | tf_op jit(solution)/shard_map/gp_grad/pallas_call | solution.py:492
  88.1 2.1 %finish.1 = (f32[128,128]{1,0:T(8,128)}, f32[128,1024]{1,0:T(8,128)}, f32[8,128]{1,0:T(8,128)}, f32[1024,128]{1,0:T(8,128)}) custom-call(f32[128,128]{1,0:T(8,128)} %get-tuple-element.10.fg_in, bf16[2,8,144,128]{3,2,1,0:T(8,128)(2,1)} %get-tuple-element.11.fin), custom_call_target="tpu_custom_call" | custom-call | tf_op jit(solution)/shard_map/finish/pallas_call | solution.py:528

commit v3 on v2

--- a/solution.py
+++ b/solution.py
@@ -26,11 +26,12 @@
 
 
 def body(
-    points, w_in, b_in, w_out, scales, left, right,
+    points_hbm, w_in_hbm, b_in, w_out_hbm, scales, left_hbm, right_hbm,
     fg_out, fin_out,
+    points, w_in, w_out, left, right, fg_buf,
     slope, hid_t, pts_t, rows, cols, rg, rb, ni, acc, sw, t_send, t_in,
     g, x_in, s1, in1, in2, in3, fin,
-    send_y, recv_y, send_x, send_z, recv_a, send_p, recv_p,
+    load, store, send_y, recv_y, send_x, send_d, send_z, recv_a, recv_r, send_p, recv_p,
     send_t, recv_t, send_c, recv_c, send_1, recv_1, send_2, recv_2, send_3, recv_3, send_4, recv_4,
 ):
     blk = lax.axis_index("blk")
@@ -62,6 +63,15 @@
             src_ref=src, dst_ref=dst, send_sem=ss, recv_sem=rs, device_id=device, device_id_type=MESH
         )
 
+    loads = [
+        pltpu.make_async_copy(src, dst, load.at[k])
+        for k, (src, dst) in enumerate(
+            ((points_hbm, points), (w_in_hbm, w_in), (w_out_hbm, w_out), (left_hbm, left), (right_hbm, right))
+        )
+    ]
+    for copy in loads:
+        copy.start()
+
     bar = pltpu.get_barrier_semaphore()
 
     def hello(device):
@@ -75,10 +85,13 @@
     for k in range(1, NY):
         hello(at_y((y + k) % NY))
 
+    loads[0].wait()
+    loads[1].wait()
     pts = points[...]
     pre = jnp.dot(pts, w_in[...], preferred_element_type=F32) + b_in[...]
     sig = jax.nn.sigmoid(pre)
     hidden = (pre * sig).astype(BF)
+    loads[2].wait()
     feats = jnp.dot(hidden, w_out[...], preferred_element_type=F32)
     scaled = (feats * scales[...]).astype(BF)
     sf = scaled.astype(F32)
@@ -97,6 +110,8 @@
     ).astype(BF)
     mine = cols.at[c, z, x]
     mine[0:PT, 0:D] = scaled
+    loads[3].wait()
+    loads[4].wait()
     mine[0:PT, D : 2 * D] = jnp.concatenate([left[...].astype(F32), right[...].astype(F32)], axis=0).T.astype(BF)
     mine[PT:PR, 0:D] = tail
     mine[PT:PR, D : 2 * D] = jnp.zeros((16, D), BF)
@@ -109,80 +124,36 @@
     def piece(zz, xx):
         return cols.at[c, zz, xx]
 
+    def duo(zz, h):
+        return cols.at[c, zz, pl.ds(2 * h, 2)]
+
     def arrival(zz, xx):
-        return remote(piece(zz, xx), piece(zz, xx), send_p.at[zz, xx], recv_a.at[zz, xx], partner)
-
-    def z_right(zz, xx):
-        return remote(piece(zz, xx), piece(zz, xx), send_z.at[0, zz, xx], recv_a.at[zz, xx], nxt)
-
-    def z_left(zz, xx):
-        return remote(piece(zz, xx), piece(zz, xx), send_z.at[1, zz, xx], recv_a.at[zz, xx], prv)
+        return remote(piece(zz, xx), piece(zz, xx), send_x.at[0, 0], recv_a.at[zz, xx], partner)
+
+    def z_right(zz, h):
+        return remote(duo(zz, h), duo(zz, h), send_z.at[0, zz, h], recv_r.at[zz, h], nxt)
+
+    def z_left(zz, h):
+        return remote(duo(zz, h), duo(zz, h), send_z.at[1, zz, h], recv_r.at[zz, h], prv)
 
     def z_direct(k):
-        return remote(mine, mine, send_z.at[0, k, 0], recv_a.at[z, x], at_z((z + k) % NZ))
+        return remote(mine, mine, send_d.at[k], recv_a.at[z, x], at_z((z + k) % NZ))
 
     def x_copy(zz, k):
         return remote(piece(zz, x), piece(zz, x), send_x.at[zz, k], recv_a.at[zz, x], at_x((x + k) % NX))
 
-    def to_partner(zz, xx):
-        return remote(piece(zz, xx), piece(zz, xx), send_p.at[zz, xx], recv_p.at[zz, xx], partner)
-
-    def from_partner(zz, xx):
-        return remote(cols.at[1 - c, zz, xx], cols.at[1 - c, zz, xx], send_p.at[zz, xx], recv_p.at[zz, xx], partner)
+    def to_partner(zz, h):
+        return remote(duo(zz, h), duo(zz, h), send_p.at[zz, h], recv_p.at[zz, h], partner)
+
+    def from_partner(zz, h):
+        there = cols.at[1 - c, zz, pl.ds(2 * h, 2)]
+        return remote(there, there, send_p.at[zz, h], recv_p.at[zz, h], partner)
 
     def y_copy(k):
         return remote(mine, rows.at[slot_y((8 - k) % 8)], send_y.at[k], recv_y.at[slot_y((8 - k) % 8)], at_y((y + k) % NY))
 
     def y_from(s):
         return remote(mine, rows.at[s], send_y.at[0], recv_y.at[s], partner)
-
-    @pl.when(c == 0)
-    def _():
-        z_right(z, x).start()
-        z_left(z, x).start()
-
-    for k in (1, 3, 2):
-        x_copy(z, k).start()
-    to_partner(z, x).start()
-    for k in (1, 7, 2, 6):
-        y_copy(k).start()
-
-    @pl.when(c == 1)
-    def _():
-        for k in (1, 7, 2, 6, 3, 5, 4):
-            z_direct(k).start()
-
-    rows[0] = mine[...]
-    slope[...] = sig * (1.0 + pre * (1.0 - sig))
-    hid_t[...] = hidden.astype(F32).T.astype(BF)
-    pts_t[...] = pts.astype(F32).T.astype(BF)
-    acc[...] = jnp.zeros_like(acc)
-    sw[...] = jnp.zeros_like(sw)
-
-    for k in (1, 3, 2):
-        xx = (x + k) % NX
-        arrival(z, xx).wait_recv()
-
-        @pl.when(c == 0)
-        def _():
-            z_right(z, xx).start()
-            z_left(z, xx).start()
-
-        to_partner(z, xx).start()
-
-    for k in (3, 5, 4):
-        y_copy(k).start()
-
-    def spread(zz):
-        arrival(zz, x).wait_recv()
-        for k in (1, 3, 2):
-            x_copy(zz, k).start()
-        to_partner(zz, x).start()
-
-    @pl.when(c == 1)
-    def _():
-        spread((z + NZ - 1) % NZ)
-        spread((z + 1) % NZ)
 
     def ready_rows(s):
         if s > 0:
@@ -195,7 +166,62 @@
         gf = gg.astype(F32)
         ni[at, :] = jnp.broadcast_to(0.5 * jnp.sum(gf * gf, axis=1, keepdims=True), (PT, D))
 
-    for s in range(4):
+    @pl.when(c == 0)
+    def _():
+        for k in (1, 3, 2):
+            x_copy(z, k).start()
+
+    for k in (1, 7, 2, 6):
+        y_copy(k).start()
+
+    @pl.when(c == 1)
+    def _():
+        for k in (1, 7, 2, 6, 3, 5, 4):
+            z_direct(k).start()
+
+    rows[0] = mine[...]
+    ready_rows(0)
+    slope[...] = sig * (1.0 + pre * (1.0 - sig))
+    hid_t[...] = hidden.astype(F32).T.astype(BF)
+    pts_t[...] = pts.astype(F32).T.astype(BF)
+    acc[...] = jnp.zeros_like(acc)
+    sw[...] = jnp.zeros_like(sw)
+
+    @pl.when(c == 1)
+    def _():
+        for k in (1, 3, 2):
+            x_copy(z, k).start()
+
+    own = x // 2
+
+    def ready_duo(h):
+        @pl.when(c == 0)
+        def _():
+            z_right(z, h).start()
+            z_left(z, h).start()
+
+        to_partner(z, h).start()
+
+    arrival(z, x + 1 - 2 * (x % 2)).wait_recv()
+    ready_duo(own)
+    for i in (0, 1):
+        arrival(z, 2 * (1 - own) + i).wait_recv()
+    ready_duo(1 - own)
+
+    for k in (3, 5, 4):
+        y_copy(k).start()
+
+    def spread(zz):
+        arrival(zz, x).wait_recv()
+        for k in (1, 3, 2):
+            x_copy(zz, k).start()
+
+    @pl.when(c == 1)
+    def _():
+        spread((z + NZ - 1) % NZ)
+        spread((z + 1) % NZ)
+
+    for s in range(1, 4):
         ready_rows(s)
 
     def block_of(t, way):
@@ -213,18 +239,14 @@
             for way in (0, 1):
                 zz, h = block_of(t, way)
                 on = jnp.logical_or(dist + 1 < 4, jnp.logical_and(dist == 3, h == way))
-                for i in (0, 1):
-                    xx = 2 * h + i
-                    arrival(zz, xx).wait_recv()
-
-                    @pl.when(on)
-                    def _():
-                        if way == 0:
-                            z_right(zz, xx).start()
-                        else:
-                            z_left(zz, xx).start()
-
-                    to_partner(zz, xx).start()
+                hop = z_right(zz, h) if way == 0 else z_left(zz, h)
+                hop.wait_recv()
+
+                @pl.when(on)
+                def _():
+                    hop.start()
+
+                to_partner(zz, h).start()
 
         @pl.when(c == 1)
         def _():
@@ -244,7 +266,8 @@
                     @pl.when(xx != x)
                     def _():
                         arrival(zz, xx).wait_recv()
-                        to_partner(zz, xx).start()
+
+                to_partner(zz, h).start()
 
     def tile(t, half):
         at = pl.ds(pl.multiple_of(half * HALF, HALF), HALF)
@@ -277,8 +300,7 @@
     def partner_ready(t):
         for way in (0, 1):
             zz, h = block_of(t, way)
-            for i in (0, 1):
-                from_partner(zz, 2 * h + i).wait_recv()
+            from_partner(zz, h).wait_recv()
 
     def dist_of(s):
         return (0, 7, 1, 6, 2, 5, 3, 4)[s]
@@ -294,17 +316,17 @@
         return remote(t_send.at[s], t_in.at[there], send_t.at[s], recv_t.at[there], at_y((y + k) % NY))
 
     def main(j, carry):
-        t = jnp.where(j < 3, j, jnp.where(j < 6, j - 3, jnp.where(j < 12, 3 + (j - 6) // 2, 6 + (j - 12) % 2)))
-        half = jnp.where(j < 3, 0, jnp.where(j < 6, 1, jnp.where(j < 12, j % 2, 1 - (j - 12) // 2)))
+        t = jnp.where(j < 3, j, jnp.where(j < 6, j - 3, 3 + (j - 6) // 2))
+        half = jnp.where(j < 3, 0, jnp.where(j < 6, 1, jnp.where(j < 14, j % 2, 15 - j)))
         even = j % 2 == 0
-        first = jnp.logical_or(j < 3, jnp.logical_or(jnp.logical_and(jnp.logical_and(j >= 6, j < 12), even), jnp.logical_or(j == 12, j == 13)))
+        first = jnp.logical_or(j < 3, jnp.logical_and(j >= 6, even))
 
         @pl.when(j == 3)
         def _():
             for s in range(4, 8):
                 ready_rows(s)
 
-        @pl.when(j == 14)
+        @pl.when(j == 15)
         def _():
             for s in (7, 6, 5, 4):
                 t_send[s] = part(s).astype(BF)
@@ -336,7 +358,9 @@
         total += t_in[s].astype(F32)
 
     fg = total * scales[...]
-    fg_out[...] = fg
+    fg_buf[...] = fg
+    fg_copy = pltpu.make_async_copy(fg_buf, fg_out, store.at[0])
+    fg_copy.start()
     fgb = fg.astype(BF)
     part_out = jnp.dot(hid_t[...], fgb, preferred_element_type=F32).astype(BF)
     pg = lax.dot_general(fgb, w_out[...], NT, preferred_element_type=F32) * slope[...]
@@ -366,74 +390,60 @@
     me1 = jnp.where(c == 0, z, y)
     me2 = jnp.where(c == 0, y, z)
 
-    def packed(v):
-        b = jnp.sum(v[PT : PT + 8], axis=0, keepdims=True)
-        return v[0:PT].astype(BF), bias_tile(jnp.broadcast_to(b, (16, D)))
-
-    half_copy = remote(g.at[1 - c], x_in, send_c.at[0], recv_c.at[0], partner)
-    half_copy.start()
-    half_copy.wait_recv()
-
-    def combine(k, carry):
-        a, b = packed(g[c, k].astype(F32) + x_in[k].astype(F32))
-        s1[k, 0:PT] = a
-        s1[k, PT:PR] = b
-        return carry
-
-    lax.fori_loop(0, 8, combine, 0)
+    cuts = (pl.ds(0, 64), pl.ds(64, PR - 64))
+
+    def put(ref, q, v):
+        if q == 0:
+            ref[0:64] = v.astype(BF)
+        else:
+            ref[64:PT] = v[0:64].astype(BF)
+            ref[PT:PR] = bias_tile(jnp.broadcast_to(jnp.sum(v[64:72], axis=0, keepdims=True), (16, D)))
+
+    def total_of(slots, n, q):
+        tot = slots[0, cuts[q]].astype(F32)
+        for k in range(1, n):
+            tot += slots[k, cuts[q]].astype(F32)
+        return tot
+
+    def halves(q):
+        return remote(g.at[1 - c, :, cuts[q]], x_in.at[:, cuts[q]], send_c.at[q], recv_c.at[q], partner)
+
+    def outs(q):
+        return remote(fin.at[c, :, cuts[q]], fin.at[c, :, cuts[q]], send_c.at[2 + q], recv_c.at[2 + q], partner)
+
+    def outs_in(q):
+        return remote(fin.at[1 - c, :, cuts[q]], fin.at[1 - c, :, cuts[q]], send_c.at[2 + q], recv_c.at[2 + q], partner)
 
     def line(peers, me, n, src_of, slots, ss, rs):
-        def go(k, carry):
+        def copy(q, k):
             to = (me + k) % n
-            remote(src_of(to), slots.at[me], ss.at[k], rs.at[me], peers(to)).start()
-            return carry
-
-        def come(k, carry):
+            return remote(src_of(to).at[cuts[q]], slots.at[me, cuts[q]], ss.at[q, k], rs.at[q, me], peers(to))
+
+        def source(q, k):
             at = (me + k) % n
-            remote(src_of(at), slots.at[at], ss.at[k], rs.at[at], peers(at)).wait_recv()
-            return carry
-
-        def sent(k, carry):
-            to = (me + k) % n
-            remote(src_of(to), slots.at[me], ss.at[k], rs.at[me], peers(to)).wait_send()
-            return carry
-
-        lax.fori_loop(1, n, go, 0)
-        return lambda: lax.fori_loop(1, n, come, 0), lambda: lax.fori_loop(1, n, sent, 0)
-
-    come, sent1 = line(at_1, me1, 8, lambda k: s1.at[k], in1, send_1, recv_1)
-    in1[me1] = s1[me1]
-    come()
-    tot = in1[0].astype(F32)
-    for k in range(1, 8):
-        tot += in1[k].astype(F32)
-    a, b = packed(tot)
-    in2[me2, 0:PT] = a
-    in2[me2, PT:PR] = b
-    come, sent2 = line(at_2, me2, 8, lambda k: in2.at[me2], in2, send_2, recv_2)
-    come()
-    tot = in2[0].astype(F32)
-    for k in range(1, 8):
-        tot += in2[k].astype(F32)
-    a, b = packed(tot)
-    in3[x, 0:PT] = a
-    in3[x, PT:PR] = b
-    come, sent3 = line(at_x, x, NX, lambda k: in3.at[x], in3, send_3, recv_3)
-    come()
-    tot = in3[0].astype(F32)
-    for k in range(1, NX):
-        tot += in3[k].astype(F32)
-    a, b = packed(tot)
-    fin[c, me1, 0:PT] = a
-    fin[c, me1, PT:PR] = b
-    come, sent4 = line(at_1, me1, 8, lambda k: fin.at[c, me1], fin.at[c], send_4, recv_4)
-    come()
-    out_copy = remote(fin.at[c], fin.at[c], send_c.at[1], recv_c.at[1], partner)
-    out_copy.start()
-    remote(fin.at[1 - c], fin.at[1 - c], send_c.at[1], recv_c.at[1], partner).wait_recv()
-
-    fin_out[...] = fin[...]
-
+            return remote(src_of(at).at[cuts[q]], slots.at[at, cuts[q]], ss.at[q, k], rs.at[q, at], peers(at))
+
+        def go(q):
+            for k in range(1, n):
+                copy(q, k).start()
+
+        def come(q):
+            for k in range(1, n):
+                source(q, k).wait_recv()
+
+        def sent():
+            for q in (0, 1):
+                for k in range(1, n):
+                    copy(q, k).wait_send()
+
+        return go, come, sent
+
+    go1, come1, sent1 = line(at_1, me1, 8, lambda k: s1.at[k], in1, send_1, recv_1)
+    go2, come2, sent2 = line(at_2, me2, 8, lambda k: in2.at[me2], in2, send_2, recv_2)
+    go3, come3, sent3 = line(at_x, x, NX, lambda k: in3.at[x], in3, send_3, recv_3)
+    go4, come4, sent4 = line(at_1, me1, 8, lambda k: fin.at[c, me1], fin.at[c], send_4, recv_4)
+    for q in (0, 1):
+        halves(q).start()
     for k in (1, 3, 2):
         x_copy(z, k).wait_send()
     for k in range(1, 8):
@@ -441,24 +451,24 @@
         t_copy(k).wait_send()
 
     def sent(i, carry):
-        zz, xx = i // NX, i % NX
+        zz, h = i // 2, i % 2
         back = (z + NZ - zz) % NZ
         ahead = (zz + NZ - z) % NZ
 
         @pl.when(c == 0)
         def _():
-            @pl.when(jnp.logical_or(back < 3, jnp.logical_and(back == 3, xx < 2)))
+            @pl.when(jnp.logical_or(back < 3, jnp.logical_and(back == 3, h == 0)))
             def _():
-                z_right(zz, xx).wait_send()
-
-            @pl.when(jnp.logical_or(ahead < 3, jnp.logical_and(ahead == 3, xx >= 2)))
+                z_right(zz, h).wait_send()
+
+            @pl.when(jnp.logical_or(ahead < 3, jnp.logical_and(ahead == 3, h == 1)))
             def _():
-                z_left(zz, xx).wait_send()
-
-        to_partner(zz, xx).wait_send()
+                z_left(zz, h).wait_send()
+
+        to_partner(zz, h).wait_send()
         return carry
 
-    lax.fori_loop(0, NZ * NX, sent, 0)
+    lax.fori_loop(0, NZ * 2, sent, 0)
 
     @pl.when(c == 1)
     def _():
@@ -467,12 +477,43 @@
             for m in (1, 3, 2):
                 x_copy((z + k) % NZ, m).wait_send()
 
-    half_copy.wait_send()
-    out_copy.wait_send()
+    for q in (0, 1):
+        halves(q).wait_recv()
+        for k in range(8):
+            put(s1.at[k], q, g[c, k, cuts[q]].astype(F32) + x_in[k, cuts[q]].astype(F32))
+        in1[me1, cuts[q]] = s1[me1, cuts[q]]
+        go1(q)
+    for q in (0, 1):
+        come1(q)
+        put(in2.at[me2], q, total_of(in1, 8, q))
+        go2(q)
     sent1()
+    for q in (0, 1):
+        halves(q).wait_send()
+    for q in (0, 1):
+        come2(q)
+        put(in3.at[x], q, total_of(in2, 8, q))
+        go3(q)
     sent2()
+    for q in (0, 1):
+        come3(q)
+        put(fin.at[c, me1], q, total_of(in3, NX, q))
+        go4(q)
     sent3()
+    for q in (0, 1):
+        come4(q)
+        outs(q).start()
+    for q in (0, 1):
+        outs_in(q).wait_recv()
+
+    fin_copy = pltpu.make_async_copy(fin, fin_out, store.at[1])
+    fin_copy.start()
+    fg_copy.wait()
+    fin_copy.wait()
+
     sent4()
+    for q in (0, 1):
+        outs(q).wait_send()
 
 
 def finish(fg_in, fin, fg_out, gi_out, gb_out, go_out):
@@ -487,6 +528,7 @@
 
 def local(points, w_in, b_in, w_out, scales, left, right):
     vmem = pl.BlockSpec(memory_space=pltpu.VMEM)
+    hbm = pl.BlockSpec(memory_space=pl.ANY)
     dma = pltpu.SemaphoreType.DMA
     piece = (PR, D)
     fg, sums = pl.pallas_call(
@@ -495,9 +537,15 @@
             jax.ShapeDtypeStruct((PT, D), F32),
             jax.ShapeDtypeStruct((2, 8) + piece, BF),
         ],
-        in_specs=[vmem] * 7,
-        out_specs=[vmem] * 2,
+        in_specs=[hbm, hbm, vmem, hbm, vmem, hbm, hbm],
+        out_specs=[hbm] * 2,
         scratch_shapes=[
+            pltpu.VMEM((PT, D), BF),
+            pltpu.VMEM((D, HID), BF),
+            pltpu.VMEM((HID, D), BF),
+            pltpu.VMEM((64, PT), BF),
+            pltpu.VMEM((64, PT), BF),
+            pltpu.VMEM((PT, D), F32),
             pltpu.VMEM((PT, HID), F32),
             pltpu.VMEM((HID, PT), BF),
             pltpu.VMEM((D, PT), BF),
@@ -517,10 +565,10 @@
             pltpu.VMEM((8,) + piece, BF),
             pltpu.VMEM((NX,) + piece, BF),
             pltpu.VMEM((2, 8) + piece, BF),
-            dma((8,)), dma((8,)), dma((NZ, NX)),
-            dma((2, NZ, NX)), dma((NZ, NX)), dma((NZ, NX)), dma((NZ, NX)),
-            dma((8,)), dma((8,)), dma((2,)), dma((2,)),
-            dma((8,)), dma((8,)), dma((8,)), dma((8,)), dma((4,)), dma((4,)), dma((8,)), dma((8,)),
+            dma((5,)), dma((2,)), dma((8,)), dma((8,)), dma((NZ, NX)),
+            dma((8,)), dma((2, NZ, 2)), dma((NZ, NX)), dma((NZ, 2)), dma((NZ, 2)), dma((NZ, 2)),
+            dma((8,)), dma((8,)), dma((4,)), dma((4,)),
+            dma((2, 8)), dma((2, 8)), dma((2, 8)), dma((2, 8)), dma((2, 4)), dma((2, 4)), dma((2, 8)), dma((2, 8)),
         ],
         compiler_params=pltpu.CompilerParams(collective_id=0, has_side_effects=True),
         name="gp_grad",

time: 90.3 us -> 87.1 us (0.965)
  Pallas kernels: 89.5 us -> 86.3 us
    pallas_call x1, Pallas kernels: 87.4 us -> 84.1 us  [local(): pl.pallas_call(body, out_shape=[jax.ShapeDtypeStruct((PT, D), F32), jax.S...]
where the time goes in v3:
time: 87.1 us; the launch traced here: 86.9 us
  Pallas kernels  86.3 us (99%)
    pallas_call x1, Pallas kernels, local(): pl.pallas_call(body, out_shape=[jax.ShapeDtypeStruct((PT, D), F32), jax.S...  84.1 us
    pallas_call x1, Pallas kernels, local(): pl.pallas_call(finish, out_shape=[jax.ShapeDtypeStruct((PT, D), F32), jax...  2.13 us

profile of v3, /device:TPU:1, one launch (start us, length us, event | category | flops | bytes accessed | tf_op | source)
XLA Modules:
  0.0 86.9 jit_solution(12690046612536128929)
XLA Ops:
  0.6 84.1 %gp_grad.1 = (f32[128,128]{1,0:T(8,128)}, bf16[2,8,144,128]{3,2,1,0:T(8,128)(2,1)}) custom-call(bf16[128,128]{1,0:T(8,128)(2,1)} %points_hbm.1, bf16[128,1024]{1,0:T(8,128)(2,1)} %w_in_hbm.1, f32[1,1024]{1,0:T(1,128)} %bitcast.7, bf16[1024,128]{1,0:T(8,128)(2,1)} %w_out_hbm.1, f32[1,128]{1,0:T(1,128)} %bitcast.8, bf16[64,128]{1,0:T(8,128)(2,1)} %bitcast.5, ...), custom_call_target="tpu_custom_call" | custom-call | tf_op jit(solution)/shard_map/gp_grad/pallas_call | solution.py:534
  84.8 2.1 %finish.1 = (f32[128,128]{1,0:T(8,128)}, f32[128,1024]{1,0:T(8,128)}, f32[8,128]{1,0:T(8,128)}, f32[1024,128]{1,0:T(8,128)}) custom-call(f32[128,128]{1,0:T(8,128)} %get-tuple-element.10.fg_in, bf16[2,8,144,128]{3,2,1,0:T(8,128)(2,1)} %get-tuple-element.11.fin), custom_call_target="tpu_custom_call" | custom-call | tf_op jit(solution)/shard_map/finish/pallas_call | solution.py:576

commit v4 on v3

--- a/solution.py
+++ b/solution.py
@@ -136,8 +136,8 @@
     def z_left(zz, h):
         return remote(duo(zz, h), duo(zz, h), send_z.at[1, zz, h], recv_r.at[zz, h], prv)
 
-    def z_direct(k):
-        return remote(mine, mine, send_d.at[k], recv_a.at[z, x], at_z((z + k) % NZ))
+    def z_one(way, zz):
+        return remote(piece(zz, x), piece(zz, x), send_d.at[way, zz], recv_a.at[zz, x], prv if way else nxt)
 
     def x_copy(zz, k):
         return remote(piece(zz, x), piece(zz, x), send_x.at[zz, k], recv_a.at[zz, x], at_x((x + k) % NX))
@@ -171,13 +171,13 @@
         for k in (1, 3, 2):
             x_copy(z, k).start()
 
-    for k in (1, 7, 2, 6):
+    for k in (1, 7, 2, 6, 3, 5, 4):
         y_copy(k).start()
 
     @pl.when(c == 1)
     def _():
-        for k in (1, 7, 2, 6, 3, 5, 4):
-            z_direct(k).start()
+        z_one(0, z).start()
+        z_one(1, z).start()
 
     rows[0] = mine[...]
     ready_rows(0)
@@ -208,21 +208,31 @@
         arrival(z, 2 * (1 - own) + i).wait_recv()
     ready_duo(1 - own)
 
-    for k in (3, 5, 4):
-        y_copy(k).start()
-
-    def spread(zz):
+
+    def spread(way, dist):
+        zz = (z + dist) % NZ if way else (z + NZ - dist) % NZ
         arrival(zz, x).wait_recv()
+
+        @pl.when(jnp.logical_or(dist < 3, jnp.logical_and(dist == 3, x % 2 == way)))
+        def _():
+            z_one(way, zz).start()
+
         for k in (1, 3, 2):
             x_copy(zz, k).start()
 
     @pl.when(c == 1)
     def _():
-        spread((z + NZ - 1) % NZ)
-        spread((z + 1) % NZ)
+        spread(0, 1)
+        spread(1, 1)
 
     for s in range(1, 4):
         ready_rows(s)
+
+    @pl.when(c == 1)
+    def _():
+        spread(0, 2)
+        spread(1, 2)
+
 
     def block_of(t, way):
         edge = jnp.logical_or(t == 0, t == 7)
@@ -250,13 +260,14 @@
 
         @pl.when(c == 1)
         def _():
-            @pl.when(t < 4)
+            @pl.when(t == 2)
             def _():
-                spread((z + NZ - (t + 1)) % NZ)
-
-            @pl.when(t < 3)
+                spread(0, 3)
+                spread(1, 3)
+
+            @pl.when(t == 4)
             def _():
-                spread((z + t + 1) % NZ)
+                spread(0, 4)
 
             for way in (0, 1):
                 zz, h = block_of(t, way)
@@ -316,17 +327,17 @@
         return remote(t_send.at[s], t_in.at[there], send_t.at[s], recv_t.at[there], at_y((y + k) % NY))
 
     def main(j, carry):
-        t = jnp.where(j < 3, j, jnp.where(j < 6, j - 3, 3 + (j - 6) // 2))
-        half = jnp.where(j < 3, 0, jnp.where(j < 6, 1, jnp.where(j < 14, j % 2, 15 - j)))
+        t = jnp.where(j < 3, j, jnp.where(j < 6, j - 3, jnp.where(j < 12, 3 + (j - 6) // 2, 6 + j % 2)))
+        half = jnp.where(j < 3, 0, jnp.where(j < 6, 1, jnp.where(j < 12, j % 2, 1 - (j - 12) // 2)))
         even = j % 2 == 0
-        first = jnp.logical_or(j < 3, jnp.logical_and(j >= 6, even))
+        first = jnp.logical_or(j < 3, jnp.logical_or(jnp.logical_and(jnp.logical_and(j >= 6, j < 12), even), jnp.logical_or(j == 12, j == 13)))
 
         @pl.when(j == 3)
         def _():
             for s in range(4, 8):
                 ready_rows(s)
 
-        @pl.when(j == 15)
+        @pl.when(j == 14)
         def _():
             for s in (7, 6, 5, 4):
                 t_send[s] = part(s).astype(BF)
@@ -472,8 +483,15 @@
 
     @pl.when(c == 1)
     def _():
+        for way in (0, 1):
+            for d in range(3):
+                z_one(way, (z + d) % NZ if way else (z + NZ - d) % NZ).wait_send()
+
+            @pl.when(x % 2 == way)
+            def _():
+                z_one(way, (z + 3) % NZ if way else (z + NZ - 3) % NZ).wait_send()
+
         for k in range(1, NZ):
-            z_direct(k).wait_send()
             for m in (1, 3, 2):
                 x_copy((z + k) % NZ, m).wait_send()
 
@@ -566,7 +584,7 @@
             pltpu.VMEM((NX,) + piece, BF),
             pltpu.VMEM((2, 8) + piece, BF),
             dma((5,)), dma((2,)), dma((8,)), dma((8,)), dma((NZ, NX)),
-            dma((8,)), dma((2, NZ, 2)), dma((NZ, NX)), dma((NZ, 2)), dma((NZ, 2)), dma((NZ, 2)),
+            dma((2, NZ)), dma((2, NZ, 2)), dma((NZ, NX)), dma((NZ, 2)), dma((NZ, 2)), dma((NZ, 2)),
             dma((8,)), dma((8,)), dma((4,)), dma((4,)),
             dma((2, 8)), dma((2, 8)), dma((2, 8)), dma((2, 8)), dma((2, 4)), dma((2, 4)), dma((2, 8)), dma((2, 8)),
         ],

time: 87.1 us -> 86.5 us (level)
  no operation moved by 1% of the time
where the time goes in v4:
time: 86.5 us; the launch traced here: 86.3 us
  Pallas kernels  85.6 us (99%)
    pallas_call x1, Pallas kernels, local(): pl.pallas_call(body, out_shape=[jax.ShapeDtypeStruct((PT, D), F32), jax.S...  83.5 us
    pallas_call x1, Pallas kernels, local(): pl.pallas_call(finish, out_shape=[jax.ShapeDtypeStruct((PT, D), F32), jax...  2.13 us

profile of v4, /device:TPU:1, one launch (start us, length us, event | category | flops | bytes accessed | tf_op | source)
XLA Modules:
  0.0 86.3 jit_solution(12377726471487282137)
XLA Ops:
  0.6 83.5 %gp_grad.1 = (f32[128,128]{1,0:T(8,128)}, bf16[2,8,144,128]{3,2,1,0:T(8,128)(2,1)}) custom-call(bf16[128,128]{1,0:T(8,128)(2,1)} %points_hbm.1, bf16[128,1024]{1,0:T(8,128)(2,1)} %w_in_hbm.1, f32[1,1024]{1,0:T(1,128)} %bitcast.7, bf16[1024,128]{1,0:T(8,128)(2,1)} %w_out_hbm.1, f32[1,128]{1,0:T(1,128)} %bitcast.8, bf16[64,128]{1,0:T(8,128)(2,1)} %bitcast.5, ...), custom_call_target="tpu_custom_call" | custom-call | tf_op jit(solution)/shard_map/gp_grad/pallas_call | solution.py:552
  84.1 2.1 %finish.1 = (f32[128,128]{1,0:T(8,128)}, f32[128,1024]{1,0:T(8,128)}, f32[8,128]{1,0:T(8,128)}, f32[1024,128]{1,0:T(8,128)}) custom-call(f32[128,128]{1,0:T(8,128)} %get-tuple-element.10.fg_in, bf16[2,8,144,128]{3,2,1,0:T(8,128)(2,1)} %get-tuple-element.11.fin), custom_call_target="tpu_custom_call" | custom-call | tf_op jit(solution)/shard_map/finish/pallas_call | solution.py:594
